TPU v7x, 32 devices: a whole 2x2x4 slice. The times are simulated.
32 devices in a mesh: dp: 8 (over z, y), tensor: 4 (over x, core).
Axes of the slice: x: 2, y: 2, z: 4, core: 2. Of those that a mesh axis runs over, the one named last changes fastest.
Arguments:
- tokens: bfloat16 [8192, 768], P(('dp', 'tensor')), may hold values from -6 to 6
- cotangent: bfloat16 [8192, 768], P(('dp', 'tensor')), may hold values from -6 to 6
- segments: int32 [8192], P('dp'), may hold values from 0 to 95, as said below
- lengths: int32 [32, 2], P('dp'), may hold values from 2 to 197, as said below
- rel_index: int32 [8192, 256], P('dp'), may hold values from 0 to 731, as said below
- w_qkv: bfloat16 [2, 768, 3, 768], P(None, None, None, 'tensor'), may hold values from -0.21875 to 0.21875
- qv_bias: bfloat16 [2, 2, 768], P(None, None, 'tensor'), may hold values from -3 to 3
- w_out: bfloat16 [2, 768, 768], P(None, 'tensor'), may hold values from -0.875 to 0.875
- w_fc1: bfloat16 [2, 768, 3072], P(None, None, 'tensor'), may hold values from -0.21875 to 0.21875
- fc1_bias: bfloat16 [2, 3072], P(None, 'tensor'), may hold values from -3 to 3
- w_fc2: bfloat16 [2, 3072, 768], P(None, 'tensor'), may hold values from -0.109375 to 0.109375
- rel_table: bfloat16 [2, 732, 12], P(None, None, 'tensor'), may hold values from -5 to 5
- ln_gain: float32 [2, 2, 768], replicated, may hold values from 0.25 to 1.75
- ln_bias: float32 [2, 2, 768], replicated, may hold values from -2 to 2
- layer_scale: float32 [2, 2, 768], replicated, may hold values from 0.25 to 1.75
- row_bias: float32 [2, 2, 768], replicated, may hold values from -2 to 2
Outputs:
- result: bfloat16 [8192, 768], P(('dp', 'tensor'))
- d_tokens: float32 [8192, 768], P(('dp', 'tensor'))
- d_w_qkv: float32 [2, 768, 3, 768], P(None, None, None, 'tensor')
- d_qv_bias: float32 [2, 2, 768], P(None, None, 'tensor')
- d_w_out: float32 [2, 768, 768], P(None, 'tensor')
- d_w_fc1: float32 [2, 768, 3072], P(None, None, 'tensor')
- d_fc1_bias: float32 [2, 3072], P(None, 'tensor')
- d_w_fc2: float32 [2, 3072, 768], P(None, 'tensor')
- d_rel_table: float32 [2, 732, 12], P(None, None, 'tensor')
- d_ln_gain: float32 [2, 2, 768], replicated
- d_ln_bias: float32 [2, 2, 768], replicated
- d_layer_scale: float32 [2, 2, 768], replicated
- d_row_bias: float32 [2, 2, 768], replicated
Inputs may be any that keep to these rules, and one draw needn't show every extreme that they name: `segments`: rows with equal ids belong to one image, or to the padding that ends one bin of 256 rows. Bin b holds rows of id 3 b (its first image), then 3 b + 1 (its second image), then one or more rows of id 3 b + 2 (padding). `lengths`: the rows of a bin's first and second image, in the order of segments; an image of r by c patches has r c + 1 rows, its class token first, then its patches row by row; a bin's two lengths sum to 255 or less. `rel_index`: for rows i and j of one image: (dr + 13) * 27 + dc + 13 for two patches whose row and column offsets are dr and dc, 729 from the class token to a patch, 730 from a patch to the class token, 731 for the class token with itself. Other entries are arbitrary.
All inputs are finite; a program needn't handle non-finite values.
Results may differ from a plain program's by a relative error of at most 0.023.
Values may be sent and summed in bfloat16 or wider, within the bound.
A program may use at most 128 MiB of HBM per device.

v0:
```python
import math

import jax
import jax.numpy as jnp
from jax import lax
from jax.sharding import PartitionSpec as P

HEAD_DIM = 64


def norm_rows(stream, norm_gain, norm_shift):
    center = stream - jnp.mean(stream, -1, keepdims=True)
    inverse = lax.rsqrt(jnp.mean(center * center, -1, keepdims=True) + 1e-06)
    normal = center * inverse
    return (normal * norm_gain + norm_shift, normal, inverse)


def norm_back(gradient, normal, inverse, norm_gain):
    scaled = gradient * norm_gain
    centered = (
        scaled
        - jnp.mean(scaled, -1, keepdims=True)
        - normal * jnp.mean(scaled * normal, -1, keepdims=True)
    )
    return (inverse * centered, jnp.sum(gradient * normal, 0), jnp.sum(gradient, 0))


def gelu_slope(values):
    return (
        0.5 * (1.0 + lax.erf(values * 0.7071067811865476))
        + values * jnp.exp(-0.5 * values * values) * 0.3989422804014327
    )


def contract_rows(left_side, right_side):
    return lax.dot_general(
        left_side, right_side, (((0,), (0,)), ((), ())), preferred_element_type=jnp.float32
    )


def times_transposed(left_side, right_side):
    return lax.dot_general(
        left_side, right_side, (((1,), (1,)), ((), ())), preferred_element_type=jnp.float32
    )


def block_rows(amount, bin_rows):
    return math.gcd(amount, max(1, 16384 // bin_rows))


def look_up(index_rows, table_used):
    amount, bin_rows = index_rows.shape
    layer_count, entries, head_count = table_used.shape
    step_rows = block_rows(amount, bin_rows)
    index_blocks = index_rows.reshape(amount // step_rows, step_rows * bin_rows)
    columns = jnp.transpose(table_used, (0, 2, 1)).reshape(layer_count * head_count, entries)
    table_rows = lax.broadcasted_iota(jnp.int32, (entries, 1), 0)

    def one_block(index_flat):
        onehot = (table_rows == index_flat[None, :]).astype(jnp.bfloat16)
        return jnp.dot(columns, onehot, preferred_element_type=jnp.float32).astype(jnp.bfloat16)

    looked = lax.map(one_block, index_blocks)
    looked = jnp.transpose(looked, (1, 0, 2)).reshape(
        layer_count, head_count, amount // bin_rows, bin_rows, bin_rows
    )
    return jnp.transpose(looked, (0, 2, 1, 3, 4))


def table_grad(index_rows, score_grads, entries):
    amount, bin_rows = index_rows.shape
    layer_count, bin_total, head_count = (
        score_grads.shape[0],
        score_grads.shape[1],
        score_grads.shape[2],
    )
    step_rows = block_rows(amount, bin_rows)
    step_count = amount // step_rows
    index_blocks = index_rows.reshape(step_count, step_rows * bin_rows)
    pieces = jnp.transpose(score_grads, (0, 2, 1, 3, 4)).reshape(
        layer_count * head_count, step_count, step_rows * bin_rows
    )
    pieces = jnp.transpose(pieces, (1, 0, 2))
    table_rows = lax.broadcasted_iota(jnp.int32, (entries, 1), 0)

    def add_block(totals, element):
        onehot = (table_rows == element[0][None, :]).astype(jnp.bfloat16)
        return (totals + times_transposed(element[1], onehot), None)

    totals, unused_out = lax.scan(
        add_block,
        jnp.zeros((layer_count * head_count, entries), jnp.float32),
        (index_blocks, pieces),
    )
    return jnp.transpose(totals.reshape(layer_count, head_count, entries), (0, 2, 1))


def attend_scores(queries, key_rows, position_bias, same_image, head_count, score_scale):
    local_width = queries.shape[1]
    blocked = (same_image.shape[0], same_image.shape[1], head_count, local_width // head_count)
    products = jnp.einsum(
        "bqhd,bkhd->bhqk",
        queries.reshape(blocked),
        key_rows.reshape(blocked),
        preferred_element_type=jnp.float32,
    )
    return jnp.where(
        same_image[:, None],
        products * score_scale + position_bias.astype(jnp.float32),
        -1000000000.0,
    )


def attend(queries, key_rows, values, position_bias, same_image, head_count, score_scale):
    scores = attend_scores(queries, key_rows, position_bias, same_image, head_count, score_scale)
    highest = jnp.max(scores, -1, keepdims=True)
    powers = jnp.exp(scores - highest)
    totals = jnp.sum(powers, -1, keepdims=True)
    weights = (powers / totals).astype(jnp.bfloat16)
    local_width = queries.shape[1]
    blocked = (same_image.shape[0], same_image.shape[1], head_count, local_width // head_count)
    mixture = jnp.einsum(
        "bhqk,bkhd->bqhd", weights, values.reshape(blocked), preferred_element_type=jnp.float32
    )
    return (mixture.reshape(queries.shape).astype(jnp.bfloat16), highest + jnp.log(totals))


def attend_back(
    queries,
    key_rows,
    values,
    position_bias,
    same_image,
    log_totals,
    grad_mix,
    head_count,
    score_scale,
):
    scores = attend_scores(queries, key_rows, position_bias, same_image, head_count, score_scale)
    weights = jnp.exp(scores - log_totals)
    local_width = queries.shape[1]
    blocked = (same_image.shape[0], same_image.shape[1], head_count, local_width // head_count)
    grad_blocked = grad_mix.reshape(blocked)
    grad_weights = jnp.einsum(
        "bqhd,bkhd->bhqk", grad_blocked, values.reshape(blocked), preferred_element_type=jnp.float32
    )
    grad_values = jnp.einsum(
        "bhqk,bqhd->bkhd",
        weights.astype(jnp.bfloat16),
        grad_blocked,
        preferred_element_type=jnp.float32,
    )
    centered = jnp.sum(weights * grad_weights, -1, keepdims=True)
    grad_scores = (weights * (grad_weights - centered)).astype(jnp.bfloat16)
    grad_query = (
        jnp.einsum(
            "bhqk,bkhd->bqhd",
            grad_scores,
            key_rows.reshape(blocked),
            preferred_element_type=jnp.float32,
        )
        * score_scale
    )
    grad_key = (
        jnp.einsum(
            "bhqk,bqhd->bkhd",
            grad_scores,
            queries.reshape(blocked),
            preferred_element_type=jnp.float32,
        )
        * score_scale
    )
    flat_shape = queries.shape
    return (
        grad_query.reshape(flat_shape).astype(jnp.bfloat16),
        grad_key.reshape(flat_shape).astype(jnp.bfloat16),
        grad_values.reshape(flat_shape).astype(jnp.bfloat16),
        grad_scores,
    )


def per_device(
    tokens,
    cotangent,
    segments,
    lengths,
    rel_index,
    w_qkv,
    qv_bias,
    w_out,
    w_fc1,
    fc1_bias,
    w_fc2,
    rel_table,
    ln_gain,
    ln_bias,
    layer_scale,
    row_bias,
):
    own_rows, width = tokens.shape
    group_rows, bin_rows = rel_index.shape
    layer_count = w_qkv.shape[0]
    entries = rel_table.shape[1]
    place = lax.axis_index("tensor")
    score_scale = float(HEAD_DIM) ** (-0.5)
    totals = jnp.sum(lengths, 1)
    inside = jnp.arange(group_rows) % bin_rows < jnp.repeat(totals, bin_rows)
    valid = lax.dynamic_slice_in_dim(inside, place * own_rows, own_rows)[:, None]
    proj_qkv, proj_bias, proj_out, proj_up, up_bias, proj_down, table_used = (
        w_qkv,
        qv_bias,
        w_out,
        w_fc1,
        fc1_bias,
        w_fc2,
        rel_table,
    )
    head_count = table_used.shape[2]
    local_width = proj_qkv.shape[3]
    bin_total = rel_index.shape[0] // bin_rows
    seg_bins = segments.reshape(bin_total, bin_rows)
    same_image = seg_bins[:, :, None] == seg_bins[:, None, :]
    position_bias = look_up(rel_index, table_used)

    def spread_rows(values):
        return lax.all_gather(values, "tensor", axis=0, tiled=True)

    def spread_grads(values):
        return lax.all_gather(values, "tensor", axis=0, tiled=True)

    def project_rows(left_side, right_side):
        return lax.psum_scatter(
            jnp.dot(left_side, right_side, preferred_element_type=jnp.float32).astype(jnp.bfloat16),
            "tensor",
            scatter_dimension=0,
            tiled=True,
        ).astype(jnp.float32)

    def project_grads(left_side, right_side):
        return lax.psum_scatter(
            times_transposed(left_side, right_side).astype(jnp.bfloat16),
            "tensor",
            scatter_dimension=0,
            tiled=True,
        ).astype(jnp.float32)

    stream = tokens.astype(jnp.float32)
    kept_state = []
    for layer_at in range(layer_count):
        layer_qkv = proj_qkv[layer_at].reshape(width, 3 * local_width)
        normed, normal_a, inverse_a = norm_rows(stream, ln_gain[layer_at, 0], ln_bias[layer_at, 0])
        spread_a = spread_rows(normed.astype(jnp.bfloat16))
        mixed_proj = jnp.dot(spread_a, layer_qkv, preferred_element_type=jnp.float32).reshape(
            -1, 3, local_width
        )
        biases = proj_bias[layer_at].astype(jnp.float32)
        queries = (mixed_proj[:, 0] + biases[0]).astype(jnp.bfloat16)
        key_rows = mixed_proj[:, 1].astype(jnp.bfloat16)
        values = (mixed_proj[:, 2] + biases[1]).astype(jnp.bfloat16)
        mixture, log_totals = attend(
            queries, key_rows, values, position_bias[layer_at], same_image, head_count, score_scale
        )
        branch_a = project_rows(mixture, proj_out[layer_at]) + row_bias[layer_at, 0]
        middle = stream + layer_scale[layer_at, 0] * branch_a
        normed_b, normal_b, inverse_b = norm_rows(
            middle, ln_gain[layer_at, 1], ln_bias[layer_at, 1]
        )
        spread_b = spread_rows(normed_b.astype(jnp.bfloat16))
        hidden = jnp.dot(spread_b, proj_up[layer_at], preferred_element_type=jnp.float32) + up_bias[
            layer_at
        ].astype(jnp.float32)
        active = jax.nn.gelu(hidden, approximate=False).astype(jnp.bfloat16)
        branch_b = project_rows(active, proj_down[layer_at]) + row_bias[layer_at, 1]
        kept_state.append(
            (
                normal_a,
                inverse_a,
                spread_a,
                queries,
                key_rows,
                values,
                mixture,
                log_totals,
                branch_a,
                normal_b,
                inverse_b,
                spread_b,
                hidden,
                active,
                branch_b,
            )
        )
        stream = middle + layer_scale[layer_at, 1] * branch_b
    result = jnp.where(valid, stream, 0.0).astype(jnp.bfloat16)
    gradient = jnp.where(valid, cotangent.astype(jnp.float32), 0.0)
    list_qkv = [None] * layer_count
    list_qvb = [None] * layer_count
    list_out = [None] * layer_count
    list_up = [None] * layer_count
    list_upb = [None] * layer_count
    list_down = [None] * layer_count
    list_scores = [None] * layer_count
    list_gain = [None] * layer_count
    list_shift = [None] * layer_count
    list_scale = [None] * layer_count
    list_rowb = [None] * layer_count
    for layer_at in reversed(range(layer_count)):
        (
            normal_a,
            inverse_a,
            spread_a,
            queries,
            key_rows,
            values,
            mixture,
            log_totals,
            branch_a,
            normal_b,
            inverse_b,
            spread_b,
            hidden,
            active,
            branch_b,
        ) = kept_state[layer_at]
        scale_b = jnp.sum(gradient * branch_b, 0)
        rowb_b = layer_scale[layer_at, 1] * jnp.sum(gradient, 0)
        spread_down = spread_grads((gradient * layer_scale[layer_at, 1]).astype(jnp.bfloat16))
        list_down[layer_at] = contract_rows(active, spread_down)
        grad_active = times_transposed(spread_down, proj_down[layer_at])
        grad_hidden = (grad_active * gelu_slope(hidden)).astype(jnp.bfloat16)
        list_upb[layer_at] = jnp.sum(grad_hidden.astype(jnp.float32), 0)
        list_up[layer_at] = contract_rows(spread_b, grad_hidden)
        back_b, gain_b, shift_b = norm_back(
            project_grads(grad_hidden, proj_up[layer_at]), normal_b, inverse_b, ln_gain[layer_at, 1]
        )
        gradient = gradient + back_b
        scale_a = jnp.sum(gradient * branch_a, 0)
        rowb_a = layer_scale[layer_at, 0] * jnp.sum(gradient, 0)
        spread_attn = spread_grads((gradient * layer_scale[layer_at, 0]).astype(jnp.bfloat16))
        list_out[layer_at] = contract_rows(mixture, spread_attn)
        grad_mix = times_transposed(spread_attn, proj_out[layer_at]).astype(jnp.bfloat16)
        grad_query, grad_key, grad_value, grad_scores = attend_back(
            queries,
            key_rows,
            values,
            position_bias[layer_at],
            same_image,
            log_totals,
            grad_mix,
            head_count,
            score_scale,
        )
        list_scores[layer_at] = grad_scores
        list_qvb[layer_at] = jnp.stack(
            [jnp.sum(grad_query.astype(jnp.float32), 0), jnp.sum(grad_value.astype(jnp.float32), 0)]
        )
        grad_proj = jnp.stack([grad_query, grad_key, grad_value], 1).reshape(-1, 3 * local_width)
        list_qkv[layer_at] = contract_rows(spread_a, grad_proj).reshape(width, 3, local_width)
        back_a, gain_a, shift_a = norm_back(
            project_grads(grad_proj, proj_qkv[layer_at].reshape(width, 3 * local_width)),
            normal_a,
            inverse_a,
            ln_gain[layer_at, 0],
        )
        gradient = gradient + back_a
        list_gain[layer_at] = jnp.stack([gain_a, gain_b])
        list_shift[layer_at] = jnp.stack([shift_a, shift_b])
        list_scale[layer_at] = jnp.stack([scale_a, scale_b])
        list_rowb[layer_at] = jnp.stack([rowb_a, rowb_b])
    qkv_all = jnp.stack(list_qkv)
    qvb_all = jnp.stack(list_qvb)
    out_all = jnp.stack(list_out)
    up_all = jnp.stack(list_up)
    upb_all = jnp.stack(list_upb)
    down_all = jnp.stack(list_down)
    table_all = table_grad(rel_index, jnp.stack(list_scores), entries)
    qkv_all, qvb_all, out_all, up_all, upb_all, down_all, table_all = lax.psum(
        (qkv_all, qvb_all, out_all, up_all, upb_all, down_all, table_all), "dp"
    )
    gain_all, shift_all, scale_all, rowb_all = lax.psum(
        (jnp.stack(list_gain), jnp.stack(list_shift), jnp.stack(list_scale), jnp.stack(list_rowb)),
        ("dp", "tensor"),
    )
    return (
        result,
        gradient,
        qkv_all,
        qvb_all,
        out_all,
        up_all,
        upb_all,
        down_all,
        table_all,
        gain_all,
        shift_all,
        scale_all,
        rowb_all,
    )


def solution(mesh):
    in_specs = (
        P(("dp", "tensor"), None),
        P(("dp", "tensor"), None),
        P("dp"),
        P("dp", None),
        P("dp", None),
        P(None, None, None, "tensor"),
        P(None, None, "tensor"),
        P(None, "tensor", None),
        P(None, None, "tensor"),
        P(None, "tensor"),
        P(None, "tensor", None),
        P(None, None, "tensor"),
        P(),
        P(),
        P(),
        P(),
    )
    out_specs = (
        P(("dp", "tensor"), None),
        P(("dp", "tensor"), None),
        P(None, None, None, "tensor"),
        P(None, None, "tensor"),
        P(None, "tensor", None),
        P(None, None, "tensor"),
        P(None, "tensor"),
        P(None, "tensor", None),
        P(None, None, "tensor"),
        P(),
        P(),
        P(),
        P(),
    )
    return jax.shard_map(
        per_device, mesh=mesh, in_specs=in_specs, out_specs=out_specs, check_vma=False
    )
```

profile of v0, /device:TPU:0, one launch (start us, length us, event | category | flops | bytes accessed | tf_op | source)
XLA Modules:
  0.0 1150.7 jit_solution(10076995145062278454)
XLA Ops:
  15.4 128.6 %while.22 = (s32[]{:T(128)}, bf16[16,6,16384]{2,1,0:T(8,128)(2,1)}, s32[16,16384]{1,0:T(8,128)S(1)}, bf16[6,732]{1,0:T(8,128)(2,1)S(1)}, s32[]{:T(128)}) while((s32[]{:T(128)}, bf16[16,6,16384]{2,1,0:T(8,128)(2,1)}, s32[16,16384]{1,0:T(8,128)S(1)}, bf16[6,732]{1,0:T(8,128)(2,1)S(1)}, s32[]{:T(128)}) %tuple.112), condition=%wide.region_4.5_spmd.clone, body=%wide.region_3.4_spmd.clone.sunk | while | flops 156008448 | bytes 467613 | solution.py:63
  174.2 29.5 %reduce-scatter.9.cloned.1.call-done = bf16[256,768]{1,0:T(8,128)(2,1)} async-done(((bf16[1024,768]{1,0:T(8,128)(2,1)}), bf16[256,768]{1,0:T(8,128)(2,1)}) %reduce-scatter.9.cloned.1.call-update) | async-done | bytes 393232 | tf_op jit(solution)/shard_map/reduce_scatter | solution.py:232
  210.2 18.4 %all-gather.11.cloned.1.call-done = bf16[1024,768]{1,0:T(8,128)(2,1)} async-done(((bf16[256,768]{1,0:T(8,128)(2,1)}), bf16[1024,768]{1,0:T(8,128)(2,1)}) %all-gather.11.cloned.1.call-update) | async-done | bytes 1572880 | tf_op jit(solution)/shard_map/all_gather | solution.py:226
  228.6 11.0 fusion.17
  243.3 28.3 %reduce-scatter.11.cloned.1.call-done = bf16[256,768]{1,0:T(8,128)(2,1)} async-done(((bf16[1024,768]{1,0:T(8,128)(2,1)}), bf16[256,768]{1,0:T(8,128)(2,1)}) %reduce-scatter.11.cloned.1.call-update) | async-done | bytes 393232 | tf_op jit(solution)/shard_map/reduce_scatter | solution.py:232
  275.6 11.0 reduce-scatter.13.cloned.1.call-start
  315.4 28.3 %reduce-scatter.13.cloned.1.call-done = bf16[256,768]{1,0:T(8,128)(2,1)} async-done(((bf16[1024,768]{1,0:T(8,128)(2,1)}), bf16[256,768]{1,0:T(8,128)(2,1)}) %reduce-scatter.13.cloned.1.call-update) | async-done | bytes 393232 | tf_op jit(solution)/shard_map/reduce_scatter | solution.py:232
  351.1 16.4 %all-gather.15.cloned.1.call-done = bf16[1024,768]{1,0:T(8,128)(2,1)} async-done(((bf16[256,768]{1,0:T(8,128)(2,1)}), bf16[1024,768]{1,0:T(8,128)(2,1)}) %all-gather.15.cloned.1.call-update) | async-done | bytes 1572880 | tf_op jit(solution)/shard_map/all_gather | solution.py:226
  367.5 11.2 fusion.20
  378.7 10.2 all-gather.17.cloned.1.call-done
  402.7 23.9 %reduce-scatter.17.cloned.1.call-done = bf16[256,768]{1,0:T(8,128)(2,1)} async-done(((bf16[1024,768]{1,0:T(8,128)(2,1)}), bf16[256,768]{1,0:T(8,128)(2,1)}) %reduce-scatter.17.cloned.1.call-update) | async-done | bytes 393232 | tf_op jit(solution)/shard_map/reduce_scatter | solution.py:240
  430.0 27.2 %reduce-scatter.15.cloned.1.call-done = bf16[256,768]{1,0:T(8,128)(2,1)} async-done(((bf16[1024,768]{1,0:T(8,128)(2,1)}), bf16[256,768]{1,0:T(8,128)(2,1)}) %reduce-scatter.15.cloned.1.call-update) | async-done | bytes 393232 | tf_op jit(solution)/shard_map/reduce_scatter | solution.py:232
  466.4 15.9 %all-gather.19.cloned.1.call-done = bf16[1024,768]{1,0:T(8,128)(2,1)} async-done(((bf16[256,768]{1,0:T(8,128)(2,1)}), bf16[1024,768]{1,0:T(8,128)(2,1)}) %all-gather.19.cloned.1.call-update) | async-done | bytes 1572880 | tf_op jit(solution)/shard_map/all_gather | solution.py:229
  516.0 28.3 %reduce-scatter.19.cloned.1.call-done = bf16[256,768]{1,0:T(8,128)(2,1)} async-done(((bf16[1024,768]{1,0:T(8,128)(2,1)}), bf16[256,768]{1,0:T(8,128)(2,1)}) %reduce-scatter.19.cloned.1.call-update) | async-done | bytes 393232 | tf_op jit(solution)/shard_map/reduce_scatter | solution.py:240
  550.9 19.8 %all-gather.21.cloned.1.call-done = bf16[1024,768]{1,0:T(8,128)(2,1)} async-done(((bf16[256,768]{1,0:T(8,128)(2,1)}), bf16[1024,768]{1,0:T(8,128)(2,1)}) %all-gather.21.cloned.1.call-update) | async-done | bytes 1572880 | tf_op jit(solution)/shard_map/all_gather | solution.py:229
  580.1 28.3 %reduce-scatter.21.cloned.1.call-done = bf16[256,768]{1,0:T(8,128)(2,1)} async-done(((bf16[1024,768]{1,0:T(8,128)(2,1)}), bf16[256,768]{1,0:T(8,128)(2,1)}) %reduce-scatter.21.cloned.1.call-update) | async-done | bytes 393232 | tf_op jit(solution)/shard_map/reduce_scatter | solution.py:240
  690.2 169.5 %while.23 = (s32[]{:T(128)}, f32[6,732]{1,0:T(8,128)S(1)}, bf16[16,6,16384]{2,1,0:T(8,128)(2,1)}, s32[16,16384]{1,0:T(8,128)}, s32[]{:T(128)}, /*index=5*/s32[]{:T(128)}) while((s32[]{:T(128)}, f32[6,732]{1,0:T(8,128)S(1)}, bf16[16,6,16384]{2,1,0:T(8,128)(2,1)}, s32[16,16384]{1,0:T(8,128)}, s32[]{:T(128)}, ...), condition=%wide.region_46.47_spmd.clone, body=%wide.region_45.46_spmd.clone.sunk | while | flops 155918912 | bytes 493983 | solution.py:90
  691.5 9.5 fusion.243
  702.1 9.5 fusion.243
  712.7 9.5 fusion.243
  723.3 9.5 fusion.243
  733.8 9.5 fusion.243
  744.4 9.5 fusion.243
  755.0 9.5 fusion.243
  765.6 9.5 fusion.243
  776.1 9.5 fusion.243
  786.7 9.5 fusion.243
  797.3 9.5 fusion.243
  807.9 9.5 fusion.243
  859.9 40.7 %all-reduce.1 = (f32[2,2,192]{2,1,0:T(2,128)}, f32[2,768]{1,0:T(2,128)}, f32[2,732,3]{1,2,0:T(4,128)S(1)}) all-reduce(f32[2,2,192]{2,1,0:T(2,128)S(1)} %pad_maximum_fusion.9, f32[2,768]{1,0:T(2,128)S(1)} %copy-done.67, f32[2,732,3]{1,2,0:T(4,128)S(1)} %bitcast.278), channel_id=1, replica_groups=mesh['dp'=8,'tensor'=4] {'dp'}, use_global_device_ids=true, to_apply=%region_38.39 | all-reduce | flops 6696 | bytes 53568 | tf_op jit(solution)/shard_map/psum | solution.py:377
  902.8 40.4 %all-reduce = (f32[2,2,768]{2,1,0:T(2,128)}, f32[2,2,768]{2,1,0:T(2,128)}, f32[2,2,768]{2,1,0:T(2,128)}, f32[2,2,768]{2,1,0:T(2,128)}) all-reduce(f32[2,2,768]{2,1,0:T(2,128)S(1)} %pad_maximum_fusion.4, f32[2,2,768]{2,1,0:T(2,128)S(1)} %pad_maximum_fusion.5, ...), channel_id=1, replica_groups=mesh['dp'=8,'tensor'=4] {'dp','tensor'}, use_global_device_ids=true, to_apply=%region_52.53 | all-reduce | flops 12288 | bytes 98304 | tf_op jit(solution)/shard_map/psum | solution.py:380
  945.4 187.2 %all-reduce.5.cloned.1.call-done = (f32[2,768,3,192]{1,3,2,0:T(8,128)}, f32[2,192,768]{2,1,0:T(8,128)}, f32[2,768,768]{2,1,0:T(8,128)}, f32[2,768,768]{2,1,0:T(8,128)}) async-done(((f32[2,768,3,192]{1,3,2,0:T(8,128)}, f32[2,192,768]{2,1,0:T(8,128)}, f32[2,768,768]{2,1,0:T(8,128)}, f32[2,768,768]{2,1,0:T(8,128)}), (f32[2,768,3,192]{1,3,2,0:T(8,128)}, f32[2,192,768]{2,1,0:T(8,128)}, f32[2,768,768]{2,1,0:T(8,128)}, ...) | async-done | bytes 14155792 | tf_op jit(solution)/shard_map/psum | solution.py:377
  (519 shorter events, 445.1 us)
Async XLA Ops:
  7.2 340.6 %copy-start = (s32[4,2]{0,1:T(2,128)S(1)}, s32[4,2]{0,1:T(2,128)}, u32[]{:S(2)}) copy-start(s32[4,2]{0,1:T(2,128)} %param.23) | copy-start | bytes 100
  7.2 151.4 %all-gather.9.cloned.1.call-start = ((), (), s32[]{:S(2)}) async-start(), calls=%async_computation.8 | async-start | bytes 1966080 | tf_op jit(solution)/shard_map/all_gather | solution.py:226
  13.1 190.5 %reduce-scatter.9.cloned.1.call-start = ((), (), s32[]{:S(2)}) async-start(), calls=%async_computation.9 | async-start | bytes 1966080 | tf_op jit(solution)/shard_map/reduce_scatter | solution.py:232
  15.4 128.6 %copy-start.103 = (bf16[2,2,192]{2,1,0:T(2,128)(2,1)S(1)}, bf16[2,2,192]{2,1,0:T(2,128)(2,1)}, u32[]{:S(2)}) copy-start(bf16[2,2,192]{2,1,0:T(2,128)(2,1)} %param.26) | copy-start | bytes 4612
  172.6 56.0 %all-gather.11.cloned.1.call-start = ((), (), s32[]{:S(2)}) async-start(), calls=%async_computation.10 | async-start | bytes 1966080 | tf_op jit(solution)/shard_map/all_gather | solution.py:226
  208.8 62.8 %reduce-scatter.11.cloned.1.call-start = ((), (), s32[]{:S(2)}) async-start(), calls=%async_computation.11 | async-start | bytes 1966080 | tf_op jit(solution)/shard_map/reduce_scatter | solution.py:232
  243.3 52.2 %all-gather.13.cloned.1.call-start = ((), (), s32[]{:S(2)}) async-start(), calls=%async_computation.12 | async-start | bytes 1966080 | tf_op jit(solution)/shard_map/all_gather | solution.py:226
  275.6 68.1 %reduce-scatter.13.cloned.1.call-start = ((), (), s32[]{:S(2)}) async-start(), calls=%async_computation.13 | async-start | bytes 1966080 | tf_op jit(solution)/shard_map/reduce_scatter | solution.py:232
  315.4 52.1 %all-gather.15.cloned.1.call-start = ((), (), s32[]{:S(2)}) async-start(), calls=%async_computation.14 | async-start | bytes 1966080 | tf_op jit(solution)/shard_map/all_gather | solution.py:226
  347.7 41.2 %all-gather.17.cloned.1.call-start = ((), (), s32[]{:S(2)}) async-start(), calls=%async_computation.16 | async-start | bytes 1966080 | tf_op jit(solution)/shard_map/all_gather | solution.py:229
  351.1 75.5 %reduce-scatter.17.cloned.1.call-start = ((), (), s32[]{:S(2)}) async-start(), calls=%async_computation.17 | async-start | bytes 1966080 | tf_op jit(solution)/shard_map/reduce_scatter | solution.py:240
  398.3 58.9 %reduce-scatter.15.cloned.1.call-start = ((), (), s32[]{:S(2)}) async-start(), calls=%async_computation.15 | async-start | bytes 1966080 | tf_op jit(solution)/shard_map/reduce_scatter | solution.py:232
  402.6 79.7 %all-gather.19.cloned.1.call-start = ((), (), s32[]{:S(2)}) async-start(), calls=%async_computation.18 | async-start | bytes 1966080 | tf_op jit(solution)/shard_map/all_gather | solution.py:229
  462.6 81.7 %reduce-scatter.19.cloned.1.call-start = ((), (), s32[]{:S(2)}) async-start(), calls=%async_computation.19 | async-start | bytes 1966080 | tf_op jit(solution)/shard_map/reduce_scatter | solution.py:240
  515.9 54.8 %all-gather.21.cloned.1.call-start = ((), (), s32[]{:S(2)}) async-start(), calls=%async_computation.20 | async-start | bytes 1966080 | tf_op jit(solution)/shard_map/all_gather | solution.py:229
  550.9 57.5 %reduce-scatter.21.cloned.1.call-start = ((), (), s32[]{:S(2)}) async-start(), calls=%async_computation.21 | async-start | bytes 1966080 | tf_op jit(solution)/shard_map/reduce_scatter | solution.py:240
  580.0 56.3 %all-gather.23.cloned.1.call-start = ((), (), s32[]{:S(2)}) async-start(), calls=%async_computation.22 | async-start | bytes 1966080 | tf_op jit(solution)/shard_map/all_gather | solution.py:229
  614.8 286.4 %reduce-scatter.23.cloned.1.call-start = ((), (), s32[]{:S(2)}) async-start(), calls=%async_computation.23 | async-start | bytes 1966080 | tf_op jit(solution)/shard_map/reduce_scatter | solution.py:240
  654.3 478.3 %all-reduce.5.cloned.1.call-start = ((), (), s32[]{:S(2)}) async-start(), calls=%async_computation.24 | async-start | bytes 28311552 | tf_op jit(solution)/shard_map/psum | solution.py:377
  690.1 169.6 %copy-start.90 = (f32[3,64]{1,0:T(4,128)S(1)}, f32[3,64]{1,0:T(4,128)}, u32[]{:S(2)}) copy-start(f32[3,64]{1,0:T(4,128)} %get-tuple-element.224) | copy-start | bytes 2308
  690.1 169.6 %copy-start.95 = (f32[3,64]{1,0:T(4,128)S(1)}, f32[3,64]{1,0:T(4,128)}, u32[]{:S(2)}) copy-start(f32[3,64]{1,0:T(4,128)} %get-tuple-element.226) | copy-start | bytes 2308
  690.1 169.8 %copy-start.94 = (f32[1,2,192]{2,1,0:T(2,128)S(1)}, f32[1,2,192]{2,1,0:T(2,128)}, u32[]{:S(2)}) copy-start(f32[1,2,192]{2,1,0:T(2,128)} %maximum_bitcast_fusion.10) | copy-start | bytes 4612
  690.1 169.8 %copy-start.67 = (f32[2,768]{1,0:T(2,128)S(1)}, f32[2,768]{1,0:T(2,128)}, u32[]{:S(2)}) copy-start(f32[2,768]{1,0:T(2,128)} %pad_maximum_fusion.8) | copy-start | bytes 18436
  690.1 211.1 %copy-start.44 = (f32[768]{0:T(1024)S(1)}, f32[768]{0:T(1024)}, u32[]{:S(2)}) copy-start(f32[768]{0:T(1024)} %copy-done.43) | copy-start | bytes 9220
  690.1 211.1 %copy-start.58 = (f32[256]{0:T(256)S(1)}, f32[256]{0:T(256)}, u32[]{:S(2)}) copy-start(f32[256]{0:T(256)} %copy-done.57) | copy-start | bytes 3076
  690.1 211.1 %copy-start.69 = (f32[256]{0:T(256)S(1)}, f32[256]{0:T(256)}, u32[]{:S(2)}) copy-start(f32[256]{0:T(256)} %copy-done.68) | copy-start | bytes 3076
  690.1 212.6 %copy-start.87 = (f32[1,768]{1,0:T(1,128)S(1)}, f32[1,768]{1,0:T(1,128)}, u32[]{:S(2)}) copy-start(f32[1,768]{1,0:T(1,128)} %stack.215) | copy-start | bytes 9220
  690.1 212.6 %copy-start.88 = (f32[1,768]{1,0:T(1,128)S(1)}, f32[1,768]{1,0:T(1,128)}, u32[]{:S(2)}) copy-start(f32[1,768]{1,0:T(1,128)} %stack.224) | copy-start | bytes 9220
  690.1 212.6 %copy-start.64 = (f32[1,2,768]{2,1,0:T(2,128)S(1)}, f32[1,2,768]{2,1,0:T(2,128)}, u32[]{:S(2)}) copy-start(f32[1,2,768]{2,1,0:T(2,128)} %maximum_bitcast_fusion.2) | copy-start | bytes 18436
  690.1 212.6 %copy-start.65 = (f32[1,2,768]{2,1,0:T(2,128)S(1)}, f32[1,2,768]{2,1,0:T(2,128)}, u32[]{:S(2)}) copy-start(f32[1,2,768]{2,1,0:T(2,128)} %maximum_bitcast_fusion.4) | copy-start | bytes 18436
  690.2 212.6 %copy-start.54 = (f32[2,2,768]{2,1,0:T(2,128)S(1)}, f32[2,2,768]{2,1,0:T(2,128)}, u32[]{:S(2)}) copy-start(f32[2,2,768]{2,1,0:T(2,128)} %pad_maximum_fusion.7) | copy-start | bytes 36868
  690.2 253.1 %copy-start.12 = (f32[256,768]{1,0:T(8,128)S(1)}, f32[256,768]{1,0:T(8,128)}, u32[]{:S(2)}) copy-start(f32[256,768]{1,0:T(8,128)} %copy-done.11) | copy-start | bytes 2359300
  (105 other events, 614.8 us)
Sparse Core Ops, SparseCore 0:
  13.3 22.3 all-gather.8
  172.7 30.8 reduce-scatter.8
  208.9 19.6 all-gather.10
  243.4 28.1 reduce-scatter.10
  275.8 19.6 all-gather.12
  315.5 28.1 reduce-scatter.12
  347.8 19.6 all-gather.14
  369.2 19.7 all-gather.16
  398.4 28.1 reduce-scatter.16
  429.0 28.1 reduce-scatter.14
  462.7 19.6 all-gather.18
  516.0 28.1 reduce-scatter.18
  551.0 19.6 all-gather.20
  580.1 28.1 reduce-scatter.20
  614.9 19.6 all-gather.22
  654.4 28.1 reduce-scatter.22
  689.5 443.0 all-reduce.4
where the time goes:
time: 1160 us; the launch traced here: 1150 us
  waiting for transfers between devices  468 us (40%)
  matrix products  388 us (33%)
  local copies, waits for them, and re-layouts  124 us (11%)
  blocking collectives  81.1 us (7%)
  other arithmetic  61.5 us (5%)
  between operations  15.7 us (1%)
  starting transfers between devices  12.5 us (1%)
    psum x1, waiting for transfers between devices, per_device(): lax.psum((qkv_all, qvb_all, out_all, up_all, upb_all, down_all, table_all...  187 us
    dot_general x24, matrix products, times_transposed(): lax.dot_general(left_side, right_side, (((1,), (1,)), ((), ())), preferre...  180 us
    dot_general x16, matrix products, one_block(): jnp.dot(columns, onehot, preferred_element_type=jnp.float32)  128 us
    reduce_scatter x4, waiting for transfers between devices, project_rows(): lax.psum_scatter(jnp.dot(left_side, right_side, preferred_element_type=jn...  113 us
    reduce_scatter x4, waiting for transfers between devices, project_grads(): lax.psum_scatter(times_transposed(left_side, right_side).astype(jnp.bfloa...  80.5 us
    all_gather x4, waiting for transfers between devices, spread_grads(): return lax.all_gather(values, 'tensor', axis=0, tiled=True)  45.9 us
    all_gather x4, waiting for transfers between devices, spread_rows(): return lax.all_gather(values, 'tensor', axis=0, tiled=True)  40.9 us
    psum x1, blocking collectives, per_device(): lax.psum((qkv_all, qvb_all, out_all, up_all, upb_all, down_all, table_all...  40.7 us
  transfers between devices with their start and end apart: 17, of which 14 were waited for; matrix products, arithmetic and copies ran while one was open for 35% of the time, Pallas kernels for 0%

commit v1 on v0

--- a/solution.py
+++ b/solution.py
@@ -44,55 +44,74 @@
     )
 
 
-def block_rows(amount, bin_rows):
-    return math.gcd(amount, max(1, 16384 // bin_rows))
-
-
-def look_up(index_rows, table_used):
-    amount, bin_rows = index_rows.shape
+SIDE = 14
+STRIDE = 2 * SIDE - 1
+CELLS = SIDE * SIDE
+
+
+def place_rows(index_rows, lengths, bin_rows):
+    bin_total = lengths.shape[0]
+    index_bins = index_rows.reshape(bin_total, bin_rows, bin_rows)
+    first, both = lengths[:, 0:1], lengths[:, 0:1] + lengths[:, 1:2]
+    code_first = index_bins[:, 1]
+    code_second = jax.vmap(lambda rows, at: lax.dynamic_index_in_dim(rows, at, 0, False))(
+        index_bins, lengths[:, 0] + 1
+    )
+    at = jnp.arange(bin_rows)[None]
+    code = (SIDE - 1) * (STRIDE + 1) - jnp.where(at < first, code_first, code_second)
+    cell = (code // STRIDE) * SIDE + code % STRIDE
+    cell = jnp.where((at == 0) | (at == first), CELLS, cell)
+    cell = jnp.where(at < both, cell, bin_rows - 1)
+    return (cell[:, :, None] == jnp.arange(bin_rows)[None, None]).astype(jnp.bfloat16)
+
+
+def grid_table(table_used, bin_rows):
     layer_count, entries, head_count = table_used.shape
-    step_rows = block_rows(amount, bin_rows)
-    index_blocks = index_rows.reshape(amount // step_rows, step_rows * bin_rows)
     columns = jnp.transpose(table_used, (0, 2, 1)).reshape(layer_count * head_count, entries)
-    table_rows = lax.broadcasted_iota(jnp.int32, (entries, 1), 0)
-
-    def one_block(index_flat):
-        onehot = (table_rows == index_flat[None, :]).astype(jnp.bfloat16)
-        return jnp.dot(columns, onehot, preferred_element_type=jnp.float32).astype(jnp.bfloat16)
-
-    looked = lax.map(one_block, index_blocks)
-    looked = jnp.transpose(looked, (1, 0, 2)).reshape(
-        layer_count, head_count, amount // bin_rows, bin_rows, bin_rows
-    )
-    return jnp.transpose(looked, (0, 2, 1, 3, 4))
-
-
-def table_grad(index_rows, score_grads, entries):
-    amount, bin_rows = index_rows.shape
-    layer_count, bin_total, head_count = (
-        score_grads.shape[0],
-        score_grads.shape[1],
-        score_grads.shape[2],
-    )
-    step_rows = block_rows(amount, bin_rows)
-    step_count = amount // step_rows
-    index_blocks = index_rows.reshape(step_count, step_rows * bin_rows)
-    pieces = jnp.transpose(score_grads, (0, 2, 1, 3, 4)).reshape(
-        layer_count * head_count, step_count, step_rows * bin_rows
-    )
-    pieces = jnp.transpose(pieces, (1, 0, 2))
-    table_rows = lax.broadcasted_iota(jnp.int32, (entries, 1), 0)
-
-    def add_block(totals, element):
-        onehot = (table_rows == element[0][None, :]).astype(jnp.bfloat16)
-        return (totals + times_transposed(element[1], onehot), None)
-
-    totals, unused_out = lax.scan(
-        add_block,
-        jnp.zeros((layer_count * head_count, entries), jnp.float32),
-        (index_blocks, pieces),
-    )
-    return jnp.transpose(totals.reshape(layer_count, head_count, entries), (0, 2, 1))
+    turned = columns[:, STRIDE * STRIDE - 1 :: -1].reshape(-1, STRIDE, STRIDE)
+    by_col = jnp.stack([turned[:, :, SIDE - 1 - c : STRIDE - c] for c in range(SIDE)], 1)
+    by_row = jnp.stack([by_col[:, :, SIDE - 1 - r : STRIDE - r] for r in range(SIDE)], 1)
+    grid = by_row.reshape(-1, CELLS, CELLS)
+    grid = jnp.pad(grid, ((0, 0), (0, bin_rows - CELLS), (0, bin_rows - CELLS)))
+    row = lax.broadcasted_iota(jnp.int32, (1, bin_rows, bin_rows), 1)
+    col = lax.broadcasted_iota(jnp.int32, (1, bin_rows, bin_rows), 2)
+    last = columns[:, STRIDE * STRIDE :, None, None]
+    grid = jnp.where((row == CELLS) & (col < CELLS), last[:, 0], grid)
+    grid = jnp.where((col == CELLS) & (row < CELLS), last[:, 1], grid)
+    grid = jnp.where((row == CELLS) & (col == CELLS), last[:, 2], grid)
+    return grid.reshape(layer_count, head_count, bin_rows, bin_rows)
+
+
+def look_up(spots, grid):
+    half = jnp.einsum("bip,lhpq->lbhiq", spots, grid)
+    return jnp.einsum("lbhiq,bjq->lbhij", half, spots)
+
+
+def skew(values):
+    flipped = values[..., ::-1, :]
+    padded = jnp.pad(flipped, [(0, 0)] * (values.ndim - 1) + [(0, SIDE)])
+    flat = padded.reshape(padded.shape[:-2] + (SIDE * 2 * SIDE,))[..., : SIDE * STRIDE]
+    return jnp.sum(flat.reshape(padded.shape[:-2] + (SIDE, STRIDE)), -2)
+
+
+def table_grad(spots, score_grads, entries):
+    half = jnp.einsum("bip,lbhij->lbhpj", spots, score_grads)
+    total = jnp.einsum("lbhpj,bjq->lhpq", half, spots, preferred_element_type=jnp.float32)
+    layer_count, head_count = total.shape[:2]
+    cells = total[:, :, :CELLS, :CELLS].reshape(-1, SIDE, SIDE, SIDE, SIDE)
+    by_col = skew(jnp.transpose(cells, (0, 1, 3, 2, 4)))
+    by_both = skew(jnp.transpose(by_col, (0, 3, 1, 2)))
+    offsets = jnp.transpose(by_both, (0, 2, 1)).reshape(-1, STRIDE * STRIDE)[:, ::-1]
+    offsets = offsets.reshape(layer_count, head_count, -1)
+    tail = jnp.stack(
+        [
+            jnp.sum(total[:, :, CELLS, :CELLS], -1),
+            jnp.sum(total[:, :, :CELLS, CELLS], -1),
+            total[:, :, CELLS, CELLS],
+        ],
+        -1,
+    )
+    return jnp.transpose(jnp.concatenate([offsets, tail], -1), (0, 2, 1))
 
 
 def attend_scores(queries, key_rows, position_bias, same_image, head_count, score_scale):
@@ -220,7 +239,8 @@
     bin_total = rel_index.shape[0] // bin_rows
     seg_bins = segments.reshape(bin_total, bin_rows)
     same_image = seg_bins[:, :, None] == seg_bins[:, None, :]
-    position_bias = look_up(rel_index, table_used)
+    spots = place_rows(rel_index, lengths, bin_rows)
+    position_bias = look_up(spots, grid_table(table_used, bin_rows))
 
     def spread_rows(values):
         return lax.all_gather(values, "tensor", axis=0, tiled=True)
@@ -373,10 +393,14 @@
     up_all = jnp.stack(list_up)
     upb_all = jnp.stack(list_upb)
     down_all = jnp.stack(list_down)
-    table_all = table_grad(rel_index, jnp.stack(list_scores), entries)
-    qkv_all, qvb_all, out_all, up_all, upb_all, down_all, table_all = lax.psum(
-        (qkv_all, qvb_all, out_all, up_all, upb_all, down_all, table_all), "dp"
-    )
+    table_all = table_grad(spots, jnp.stack(list_scores), entries)
+    qvb_all, upb_all, table_all = lax.psum((qvb_all, upb_all, table_all), "dp")
+    qkv_all, out_all, up_all, down_all = [
+        total.astype(jnp.float32)
+        for total in lax.psum(
+            tuple(part.astype(jnp.bfloat16) for part in (qkv_all, out_all, up_all, down_all)), "dp"
+        )
+    ]
     gain_all, shift_all, scale_all, rowb_all = lax.psum(
         (jnp.stack(list_gain), jnp.stack(list_shift), jnp.stack(list_scale), jnp.stack(list_rowb)),
         ("dp", "tensor"),

time: 1160 us -> 840 us (0.72)
  matrix products: 388 us -> 105 us
  waiting for transfers between devices: 468 us -> 388 us
  local copies, waits for them, and re-layouts: 124 us -> 156 us
  other arithmetic: 61.5 us -> 83.4 us
    dot_general x24 -> x8, matrix products: 180 us -> 28.3 us  [times_transposed(): lax.dot_general(left_side, right_side, (((1,), (1,)), ((), ())), preferre...]
    dot_general x16 -> x3, matrix products: 128 us -> 7.3 us  [the longest x1 3.42 us: table_grad(): jnp.einsum('lbhpj,bjq->lhpq', half, spots, preferred_element_type=jnp.flo...]
    psum x1, waiting for transfers between devices: 187 us -> 80.1 us  [per_device(): lax.psum(tuple((part.astype(jnp.bfloat16) for part in (qkv_all, out_all,...]
    all_gather x4, waiting for transfers between devices: 45.9 us -> 65.1 us  [spread_grads(): return lax.all_gather(values, 'tensor', axis=0, tiled=True)]
    dynamic_slice x32 -> x0, local copies, waits for them, and re-layouts: 18.3 us -> none  [look_up(): looked = lax.map(one_block, index_blocks)]
    reshape x6 -> x11, local copies, waits for them, and re-layouts: 14 us -> 30.4 us  [the longest x2 9.27 us: skew(): return jnp.sum(flat.reshape(padded.shape[:-2] + (SIDE, STRIDE)), -2)]
    unnamed x254 -> x228, local copies, waits for them, and re-layouts: 36.6 us -> 46 us
  transfers between devices with their start and end apart: 17 -> 17, of which waited for: 14 -> 15; matrix products, arithmetic and copies ran while one was open for 35% -> 21% of each run, Pallas kernels for 0% -> 0%
where the time goes in v1:
time: 840 us; the launch traced here: 828 us
  waiting for transfers between devices  388 us (46%)
  local copies, waits for them, and re-layouts  156 us (19%)
  matrix products  105 us (12%)
  other arithmetic  83.4 us (10%)
  blocking collectives  78.3 us (9%)
  between operations  15.8 us (2%)
    reduce_scatter x4, waiting for transfers between devices, project_rows(): lax.psum_scatter(jnp.dot(left_side, right_side, preferred_element_type=jn...  113 us
    psum x1, waiting for transfers between devices, per_device(): lax.psum(tuple((part.astype(jnp.bfloat16) for part in (qkv_all, out_all,...  80.1 us
    reduce_scatter x4, waiting for transfers between devices, project_grads(): lax.psum_scatter(times_transposed(left_side, right_side).astype(jnp.bfloa...  80.1 us
    all_gather x4, waiting for transfers between devices, spread_grads(): return lax.all_gather(values, 'tensor', axis=0, tiled=True)  65.1 us
    all_gather x4, waiting for transfers between devices, spread_rows(): return lax.all_gather(values, 'tensor', axis=0, tiled=True)  49.5 us
    unnamed x228, local copies, waits for them, and re-layouts  46 us
    psum x1, blocking collectives, per_device(): lax.psum((jnp.stack(list_gain), jnp.stack(list_shift), jnp.stack(list_sca...  39.6 us
    psum x1, blocking collectives, per_device(): qvb_all, upb_all, table_all = lax.psum((qvb_all, upb_all, table_all), 'dp')  38.8 us
  transfers between devices with their start and end apart: 17, of which 15 were waited for; matrix products, arithmetic and copies ran while one was open for 21% of the time, Pallas kernels for 0%

profile of v1, /device:TPU:0, one launch (start us, length us, event | category | flops | bytes accessed | tf_op | source)
XLA Modules:
  0.0 828.0 jit_solution(12278623126363064716)
XLA Ops:
  33.6 6.6 reshape.634
  62.1 29.0 %reduce-scatter.9.cloned.1.call-done = bf16[256,768]{1,0:T(8,128)(2,1)} async-done(((bf16[1024,768]{1,0:T(8,128)(2,1)}), bf16[256,768]{1,0:T(8,128)(2,1)}) %reduce-scatter.9.cloned.1.call-update) | async-done | bytes 393232 | tf_op jit(solution)/shard_map/reduce_scatter | solution.py:252
  97.7 18.4 %all-gather.11.cloned.1.call-done = bf16[1024,768]{1,0:T(8,128)(2,1)} async-done(((bf16[256,768]{1,0:T(8,128)(2,1)}), bf16[1024,768]{1,0:T(8,128)(2,1)}) %all-gather.11.cloned.1.call-update) | async-done | bytes 1572880 | tf_op jit(solution)/shard_map/all_gather | solution.py:246
  116.1 11.0 %fusion.2 = (bf16[1024,768]{1,0:T(8,128)(2,1)S(1)}, f32[1024,768]{1,0:T(8,128)}) fusion(f32[768]{0:T(1024)} %get-tuple-element.80, bf16[1024,768]{1,0:T(8,128)(2,1)} %all-gather.11.cloned.1.call-done, bf16[2,768,768]{2,1,0:T(8,128)(2,1)} %param.24), kind=kOutput, calls=%fused_computation.7 | convolution fusion | flops 1259864064 | bytes 7475200 | tf_op jit(solution)/shard_map/dot_general | solution.py:289
  130.8 28.3 %reduce-scatter.11.cloned.1.call-done = bf16[256,768]{1,0:T(8,128)(2,1)} async-done(((bf16[1024,768]{1,0:T(8,128)(2,1)}), bf16[256,768]{1,0:T(8,128)(2,1)}) %reduce-scatter.11.cloned.1.call-update) | async-done | bytes 393232 | tf_op jit(solution)/shard_map/reduce_scatter | solution.py:252
  165.8 17.1 %all-gather.13.cloned.1.call-done = bf16[1024,768]{1,0:T(8,128)(2,1)} async-done(((bf16[256,768]{1,0:T(8,128)(2,1)}), bf16[1024,768]{1,0:T(8,128)(2,1)}) %all-gather.13.cloned.1.call-update) | async-done | bytes 1572880 | tf_op jit(solution)/shard_map/all_gather | solution.py:246
  203.0 28.1 %reduce-scatter.13.cloned.1.call-done = bf16[256,768]{1,0:T(8,128)(2,1)} async-done(((bf16[1024,768]{1,0:T(8,128)(2,1)}), bf16[256,768]{1,0:T(8,128)(2,1)}) %reduce-scatter.13.cloned.1.call-update) | async-done | bytes 393232 | tf_op jit(solution)/shard_map/reduce_scatter | solution.py:252
  241.0 14.0 %all-gather.15.cloned.1.call-done = bf16[1024,768]{1,0:T(8,128)(2,1)} async-done(((bf16[256,768]{1,0:T(8,128)(2,1)}), bf16[1024,768]{1,0:T(8,128)(2,1)}) %all-gather.15.cloned.1.call-update) | async-done | bytes 1572880 | tf_op jit(solution)/shard_map/all_gather | solution.py:246
  255.0 11.2 %fusion.5 = (bf16[1024,768]{1,0:T(8,128)(2,1)}, f32[1024,768]{1,0:T(8,128)}) fusion(f32[768]{0:T(1024)} %get-tuple-element.79, bf16[1024,768]{1,0:T(8,128)(2,1)} %all-gather.15.cloned.1.call-done, bf16[2,768,768]{2,1,0:T(8,128)(2,1)} %param.24), kind=kOutput, calls=%fused_computation.10 | convolution fusion | flops 1259864064 | bytes 7475200 | tf_op jit(solution)/shard_map/dot_general | solution.py:289
  266.1 10.2 %all-gather.17.cloned.1.call-done = bf16[1024,768]{1,0:T(8,128)(2,1)} async-done(((bf16[256,768]{1,0:T(8,128)(2,1)}), bf16[1024,768]{1,0:T(8,128)(2,1)}) %all-gather.17.cloned.1.call-update) | async-done | bytes 1572880 | tf_op jit(solution)/shard_map/all_gather | solution.py:249
  276.3 5.6 convert_reduce_fusion
  285.7 4.3 convolution_convert_fusion.4
  290.1 23.9 %reduce-scatter.17.cloned.1.call-done = bf16[256,768]{1,0:T(8,128)(2,1)} async-done(((bf16[1024,768]{1,0:T(8,128)(2,1)}), bf16[256,768]{1,0:T(8,128)(2,1)}) %reduce-scatter.17.cloned.1.call-update) | async-done | bytes 393232 | tf_op jit(solution)/shard_map/reduce_scatter | solution.py:260
  317.3 27.3 %reduce-scatter.15.cloned.1.call-done = bf16[256,768]{1,0:T(8,128)(2,1)} async-done(((bf16[1024,768]{1,0:T(8,128)(2,1)}), bf16[256,768]{1,0:T(8,128)(2,1)}) %reduce-scatter.15.cloned.1.call-update) | async-done | bytes 393232 | tf_op jit(solution)/shard_map/reduce_scatter | solution.py:252
  344.6 3.7 fusion.240
  353.7 16.1 %all-gather.19.cloned.1.call-done = bf16[1024,768]{1,0:T(8,128)(2,1)} async-done(((bf16[256,768]{1,0:T(8,128)(2,1)}), bf16[1024,768]{1,0:T(8,128)(2,1)}) %all-gather.19.cloned.1.call-update) | async-done | bytes 1572880 | tf_op jit(solution)/shard_map/all_gather | solution.py:249
  399.7 3.7 convolution_convert_fusion.1
  403.5 28.3 %reduce-scatter.19.cloned.1.call-done = bf16[256,768]{1,0:T(8,128)(2,1)} async-done(((bf16[1024,768]{1,0:T(8,128)(2,1)}), bf16[256,768]{1,0:T(8,128)(2,1)}) %reduce-scatter.19.cloned.1.call-update) | async-done | bytes 393232 | tf_op jit(solution)/shard_map/reduce_scatter | solution.py:260
  438.5 19.8 %all-gather.21.cloned.1.call-done = bf16[1024,768]{1,0:T(8,128)(2,1)} async-done(((bf16[256,768]{1,0:T(8,128)(2,1)}), bf16[1024,768]{1,0:T(8,128)(2,1)}) %all-gather.21.cloned.1.call-update) | async-done | bytes 1572880 | tf_op jit(solution)/shard_map/all_gather | solution.py:249
  458.2 5.6 convert_reduce_fusion.1
  468.0 27.9 %reduce-scatter.21.cloned.1.call-done = bf16[256,768]{1,0:T(8,128)(2,1)} async-done(((bf16[1024,768]{1,0:T(8,128)(2,1)}), bf16[256,768]{1,0:T(8,128)(2,1)}) %reduce-scatter.21.cloned.1.call-update) | async-done | bytes 393232 | tf_op jit(solution)/shard_map/reduce_scatter | solution.py:260
  503.1 19.0 %all-gather.23.cloned.1.call-done = bf16[1024,768]{1,0:T(8,128)(2,1)} async-done(((bf16[256,768]{1,0:T(8,128)(2,1)}), bf16[1024,768]{1,0:T(8,128)(2,1)}) %all-gather.23.cloned.1.call-update) | async-done | bytes 1572880 | tf_op jit(solution)/shard_map/all_gather | solution.py:249
  590.5 6.7 reshape.610
  597.3 8.5 %rev.13 = f32[6,14,14,14,14]{4,2,3,1,0:T(8,128)} reverse(f32[6,14,14,14,14]{4,2,3,1,0:T(8,128)} %bitcast.407), dimensions={3} | reverse | bytes 1843968 | tf_op jit(solution)/shard_map/rev | solution.py:91
  605.8 7.8 copy.159
  613.5 4.7 pad.14.clone
  618.2 7.3 reshape.611
  627.1 8.5 %reshape.612 = f32[6,14,14,14,27]{4,3,2,1,0:T(8,128)} reshape(f32[6,14,14,378]{3,2,1,0:T(8,128)} %slice.410) | data formatting | bytes 3556224 | tf_op jit(solution)/shard_map/reshape | solution.py:94
  635.6 6.3 reduce_sum.458
  647.1 38.8 %all-reduce.5 = (f32[2,2,192]{2,1,0:T(2,128)}, f32[2,768]{1,0:T(2,128)}, f32[2,732,3]{1,2,0:T(4,128)S(1)}) all-reduce(f32[2,2,192]{2,1,0:T(2,128)S(1)} %pad_maximum_fusion.10, f32[2,768]{1,0:T(2,128)S(1)} %copy-done.60, f32[2,732,3]{1,2,0:T(4,128)S(1)} %maximum_bitcast_fusion), channel_id=1, replica_groups=mesh['dp'=8,'tensor'=4] {'dp'}, use_global_device_ids=true, to_apply=%region_36.37 | all-reduce | flops 6696 | bytes 53568 | tf_op jit(solution)/shard_map/psum | solution.py:397
  688.1 39.6 %all-reduce.4 = (f32[2,2,768]{2,1,0:T(2,128)}, f32[2,2,768]{2,1,0:T(2,128)}, f32[2,2,768]{2,1,0:T(2,128)}, f32[2,2,768]{2,1,0:T(2,128)}) all-reduce(f32[2,2,768]{2,1,0:T(2,128)S(1)} %pad_maximum_fusion.5, f32[2,2,768]{2,1,0:T(2,128)S(1)} %pad_maximum_fusion.6, ...), channel_id=1, replica_groups=mesh['dp'=8,'tensor'=4] {'dp','tensor'}, use_global_device_ids=true, to_apply=%region_52.53 | all-reduce | flops 12288 | bytes 98304 | tf_op jit(solution)/shard_map/psum | solution.py:404
  729.9 80.1 %all-reduce.9.cloned.1.call-done = (bf16[2,768,3,192]{1,3,2,0:T(8,128)(2,1)}, bf16[2,192,768]{2,1,0:T(8,128)(2,1)}, bf16[2,768,768]{2,1,0:T(8,128)(2,1)}, bf16[2,768,768]{2,1,0:T(8,128)(2,1)}) async-done(((bf16[2,768,3,192]{1,3,2,0:T(8,128)(2,1)}, bf16[2,192,768]{2,1,0:T(8,128)(2,1)}, bf16[2,768,768]{2,1,0:T(8,128)(2,1)}, bf16[2,768,768]{2,1,0:T(8,128)(2,1)}), (bf16[2,768,3,192]{1,3,2,0:T(8,128)(2,1)}, ...) | async-done | bytes 7077904 | tf_op jit(solution)/shard_map/psum | solution.py:400
  (461 shorter events, 245.1 us)
Async XLA Ops:
  7.2 38.7 %all-gather.9.cloned.1.call-start = ((), (), s32[]{:S(2)}) async-start(), calls=%async_computation.8 | async-start | bytes 1966080 | tf_op jit(solution)/shard_map/all_gather | solution.py:246
  13.1 77.9 %reduce-scatter.9.cloned.1.call-start = ((), (), s32[]{:S(2)}) async-start(), calls=%async_computation.9 | async-start | bytes 1966080 | tf_op jit(solution)/shard_map/reduce_scatter | solution.py:252
  57.1 33.9 %copy-start.2 = (bf16[256,768]{1,0:T(8,128)(2,1)S(1)}, bf16[256,768]{1,0:T(8,128)(2,1)}, u32[]{:S(2)}) copy-start(bf16[256,768]{1,0:T(8,128)(2,1)} %param.16) | copy-start | bytes 1179652
  60.1 56.0 %all-gather.11.cloned.1.call-start = ((), (), s32[]{:S(2)}) async-start(), calls=%async_computation.10 | async-start | bytes 1966080 | tf_op jit(solution)/shard_map/all_gather | solution.py:246
  96.2 62.8 %reduce-scatter.11.cloned.1.call-start = ((), (), s32[]{:S(2)}) async-start(), calls=%async_computation.11 | async-start | bytes 1966080 | tf_op jit(solution)/shard_map/reduce_scatter | solution.py:252
  130.7 52.2 %all-gather.13.cloned.1.call-start = ((), (), s32[]{:S(2)}) async-start(), calls=%async_computation.12 | async-start | bytes 1966080 | tf_op jit(solution)/shard_map/all_gather | solution.py:246
  163.1 68.0 %reduce-scatter.13.cloned.1.call-start = ((), (), s32[]{:S(2)}) async-start(), calls=%async_computation.13 | async-start | bytes 1966080 | tf_op jit(solution)/shard_map/reduce_scatter | solution.py:252
  202.8 52.1 %all-gather.15.cloned.1.call-start = ((), (), s32[]{:S(2)}) async-start(), calls=%async_computation.14 | async-start | bytes 1966080 | tf_op jit(solution)/shard_map/all_gather | solution.py:246
  235.1 41.2 %all-gather.17.cloned.1.call-start = ((), (), s32[]{:S(2)}) async-start(), calls=%async_computation.16 | async-start | bytes 1966080 | tf_op jit(solution)/shard_map/all_gather | solution.py:249
  240.9 73.0 %reduce-scatter.17.cloned.1.call-start = ((), (), s32[]{:S(2)}) async-start(), calls=%async_computation.17 | async-start | bytes 1966080 | tf_op jit(solution)/shard_map/reduce_scatter | solution.py:260
  285.6 59.0 %reduce-scatter.15.cloned.1.call-start = ((), (), s32[]{:S(2)}) async-start(), calls=%async_computation.15 | async-start | bytes 1966080 | tf_op jit(solution)/shard_map/reduce_scatter | solution.py:252
  290.0 79.8 %all-gather.19.cloned.1.call-start = ((), (), s32[]{:S(2)}) async-start(), calls=%async_computation.18 | async-start | bytes 1966080 | tf_op jit(solution)/shard_map/all_gather | solution.py:249
  350.0 81.8 %reduce-scatter.19.cloned.1.call-start = ((), (), s32[]{:S(2)}) async-start(), calls=%async_computation.19 | async-start | bytes 1966080 | tf_op jit(solution)/shard_map/reduce_scatter | solution.py:260
  403.5 54.8 %all-gather.21.cloned.1.call-start = ((), (), s32[]{:S(2)}) async-start(), calls=%async_computation.20 | async-start | bytes 1966080 | tf_op jit(solution)/shard_map/all_gather | solution.py:249
  438.4 57.5 %reduce-scatter.21.cloned.1.call-start = ((), (), s32[]{:S(2)}) async-start(), calls=%async_computation.21 | async-start | bytes 1966080 | tf_op jit(solution)/shard_map/reduce_scatter | solution.py:260
  465.0 30.9 %copy-start.55 = (f32[256]{0:T(256)S(1)}, f32[256]{0:T(256)}, u32[]{:S(2)}) copy-start(f32[256]{0:T(256)} %copy-done.54) | copy-start | bytes 3076
  467.6 54.6 %all-gather.23.cloned.1.call-start = ((), (), s32[]{:S(2)}) async-start(), calls=%async_computation.22 | async-start | bytes 1966080 | tf_op jit(solution)/shard_map/all_gather | solution.py:249
  502.3 184.2 %reduce-scatter.23.cloned.1.call-start = ((), (), s32[]{:S(2)}) async-start(), calls=%async_computation.23 | async-start | bytes 1966080 | tf_op jit(solution)/shard_map/reduce_scatter | solution.py:260
  539.2 270.8 %all-reduce.9.cloned.1.call-start = ((), (), s32[]{:S(2)}) async-start(), calls=%async_computation.24 | async-start | bytes 14155776 | tf_op jit(solution)/shard_map/psum | solution.py:400
  558.9 19.7 %copy-start.48 = (f32[2,2,768]{2,1,0:T(2,128)S(1)}, f32[2,2,768]{2,1,0:T(2,128)}, u32[]{:S(2)}) copy-start(f32[2,2,768]{2,1,0:T(2,128)} %param.30) | copy-start | bytes 36868
  558.9 21.8 %copy-start.6 = (bf16[4,3,256,256]{2,3,1,0:T(8,128)(2,1)S(1)}, bf16[4,3,256,256]{2,3,1,0:T(8,128)(2,1)}, u32[]{:S(2)}) copy-start(bf16[4,3,256,256]{2,3,1,0:T(8,128)(2,1)} %copy-done.5) | copy-start | bytes 4718596
  558.9 21.8 %copy-start.8 = (bf16[4,3,256,256]{2,3,1,0:T(8,128)(2,1)S(1)}, bf16[4,3,256,256]{2,3,1,0:T(8,128)(2,1)}, u32[]{:S(2)}) copy-start(bf16[4,3,256,256]{2,3,1,0:T(8,128)(2,1)} %copy-done.7) | copy-start | bytes 4718596
  558.9 21.8 %copy-start.35 = (s32[4,256]{1,0:T(4,128)S(1)}, s32[4,256]{1,0:T(4,128)}, u32[]{:S(2)}) copy-start(s32[4,256]{1,0:T(4,128)} %copy-done.34) | copy-start | bytes 12292
  643.4 43.1 %copy-start.41 = (f32[768]{0:T(1024)S(1)}, f32[768]{0:T(1024)}, u32[]{:S(2)}) copy-start(f32[768]{0:T(1024)} %copy-done.40) | copy-start | bytes 9220
  643.4 43.1 %copy-start.53 = (f32[256]{0:T(256)S(1)}, f32[256]{0:T(256)}, u32[]{:S(2)}) copy-start(f32[256]{0:T(256)} %copy-done.52) | copy-start | bytes 3076
  643.4 43.1 %copy-start.62 = (f32[256]{0:T(256)S(1)}, f32[256]{0:T(256)}, u32[]{:S(2)}) copy-start(f32[256]{0:T(256)} %copy-done.61) | copy-start | bytes 3076
  643.4 44.6 %copy-start.66 = (f32[1,768]{1,0:T(1,128)S(1)}, f32[1,768]{1,0:T(1,128)}, u32[]{:S(2)}) copy-start(f32[1,768]{1,0:T(1,128)} %stack.353) | copy-start | bytes 9220
  643.4 44.6 %copy-start.67 = (f32[1,768]{1,0:T(1,128)S(1)}, f32[1,768]{1,0:T(1,128)}, u32[]{:S(2)}) copy-start(f32[1,768]{1,0:T(1,128)} %stack.362) | copy-start | bytes 9220
  643.4 44.6 %copy-start.58 = (f32[1,2,768]{2,1,0:T(2,128)S(1)}, f32[1,2,768]{2,1,0:T(2,128)}, u32[]{:S(2)}) copy-start(f32[1,2,768]{2,1,0:T(2,128)} %maximum_bitcast_fusion.2) | copy-start | bytes 18436
  643.4 44.7 %copy-start.59 = (f32[1,2,768]{2,1,0:T(2,128)S(1)}, f32[1,2,768]{2,1,0:T(2,128)}, u32[]{:S(2)}) copy-start(f32[1,2,768]{2,1,0:T(2,128)} %maximum_bitcast_fusion.4) | copy-start | bytes 18436
  643.4 44.7 %copy-start.49 = (f32[2,2,768]{2,1,0:T(2,128)S(1)}, f32[2,2,768]{2,1,0:T(2,128)}, u32[]{:S(2)}) copy-start(f32[2,2,768]{2,1,0:T(2,128)} %pad_maximum_fusion.8) | copy-start | bytes 36868
  643.4 84.2 %copy-start.10 = (f32[256,768]{1,0:T(8,128)S(1)}, f32[256,768]{1,0:T(8,128)}, u32[]{:S(2)}) copy-start(f32[256,768]{1,0:T(8,128)} %copy-done.9) | copy-start | bytes 2359300
  (78 other events, 200.0 us)
Sparse Core Ops, SparseCore 0:
  13.3 22.3 all-gather.8
  60.2 30.8 reduce-scatter.8
  96.4 19.6 all-gather.10
  130.9 28.1 reduce-scatter.10
  163.2 19.6 all-gather.12
  202.9 28.1 reduce-scatter.12
  235.3 19.6 all-gather.14
  256.6 19.6 all-gather.16
  285.7 28.1 reduce-scatter.16
  316.4 28.1 reduce-scatter.14
  350.1 19.6 all-gather.18
  403.6 28.1 reduce-scatter.18
  438.5 19.6 all-gather.20
  467.7 28.1 reduce-scatter.20
  502.4 19.6 all-gather.22
  539.3 28.1 reduce-scatter.22
  572.3 237.6 all-reduce.8

commit v2 on v1

v2 whole, which is shorter than its diff:
```python
import functools

import jax
import jax.numpy as jnp
from jax import lax
from jax.experimental import pallas as pl
from jax.experimental.pallas import tpu as pltpu
from jax.sharding import PartitionSpec as P

HEAD_DIM = 64
SIDE = 14
STRIDE = 2 * SIDE - 1
CELLS = SIDE * SIDE
PARTS = 2
CHUNK = 32
MESH = pl.DeviceIdType.MESH
BF16 = jnp.bfloat16
F32 = jnp.float32


def dot(left_side, right_side, left_axis=1, right_axis=0):
    return lax.dot_general(
        left_side,
        right_side,
        (((left_axis,), (right_axis,)), ((), ())),
        preferred_element_type=F32,
    )


class Group:
    def __init__(self, send_sems, recv_sems):
        own = lax.axis_index("tensor")
        self.near = own + 1 - 2 * (own % 2)
        self.far = (own + 2) % 4
        self.sems = (send_sems, recv_sems)

    def meet(self):
        barrier = pltpu.get_barrier_semaphore()
        for other in (self.near, self.far):
            pl.semaphore_signal(
                barrier, inc=1, device_id={"tensor": other}, device_id_type=MESH
            )
        pl.semaphore_wait(barrier, 2)

    def copy(self, at, source, target, other):
        return pltpu.make_async_remote_copy(
            src_ref=source,
            dst_ref=target,
            send_sem=self.sems[0].at[at],
            recv_sem=self.sems[1].at[at],
            device_id={"tensor": other},
            device_id_type=MESH,
        )


class Exchange:
    COPIES = 2 + 4 * PARTS

    def __init__(self, group, base, gath, part, got, summed):
        rows = gath.shape[1] // PARTS
        near, far = group.near, group.far
        self.rows = rows

        def piece(ref, slot, at):
            return ref.at[slot, pl.ds(at * rows, rows)]

        self.to_near = group.copy(base, gath.at[0], gath.at[1], near)
        self.to_far = [
            group.copy(base + 2 + at, piece(gath, 0, at), piece(gath, 2, at), far)
            for at in range(PARTS)
        ]
        self.relay = [
            group.copy(base + 2 + PARTS + at, piece(gath, 2, at), piece(gath, 3, at), near)
            for at in range(PARTS)
        ]
        self.sum_near = group.copy(base + 1, part.at[1], got.at[0], near)
        self.sum_pair = [
            group.copy(base + 2 + 2 * PARTS + at, piece(part, 3, at), piece(got, 1, at), near)
            for at in range(PARTS)
        ]
        self.sum_far = [
            group.copy(
                base + 2 + 3 * PARTS + at,
                summed.at[pl.ds(at * rows, rows)],
                piece(got, 2, at),
                far,
            )
            for at in range(PARTS)
        ]
        self.part, self.got, self.summed = part, got, summed

    def start(self):
        self.to_near.start()
        for step in self.to_far:
            step.start()

    def pass_on(self, at):
        self.to_far[at].wait_recv()
        self.relay[at].start()

    def send_sum(self, at):
        self.sum_pair[at].wait_recv()
        rows = self.rows
        span = pl.ds(at * rows, rows)
        self.summed[span] = (
            self.part[2, span].astype(F32) + self.got[1, span].astype(F32)
        ).astype(BF16)
        self.sum_far[at].start()

    def finish(self):
        self.sum_near.wait_recv()
        for step in self.sum_far:
            step.wait_recv()

    def drain(self):
        self.to_near.wait_send()
        self.sum_near.wait_send()
        for steps in (self.to_far, self.relay, self.sum_pair, self.sum_far):
            for step in steps:
                step.wait_send()


def by_chunk(total_rows, body, size=CHUNK):
    def step(at, carry):
        return body(pl.ds(pl.multiple_of(at * size, size), size), carry)

    return step, total_rows // size


def norm_chunk(values, gain, shift):
    center = values - jnp.mean(values, -1, keepdims=True)
    inverse = lax.rsqrt(jnp.mean(center * center, -1, keepdims=True) + 1e-06)
    normal = center * inverse
    return (normal * gain + shift).astype(BF16), normal, inverse


def gelu_parts(values):
    share = 0.5 * (1.0 + lax.erf(values * 0.7071067811865476))
    slope = share + values * (jnp.exp(-0.5 * values * values) * 0.3989422804014327)
    return values * share, slope


def attend_rows(qkv, weights_kept, mixture, bias, at, slot, first, head_count):
    rows = qkv.shape[2] // PARTS
    wide = qkv.shape[3] // 3
    span = pl.ds(first, rows)
    heads = []
    for head in range(head_count):
        lanes = slice(head * HEAD_DIM, (head + 1) * HEAD_DIM)
        queries = qkv[at, slot, span, 0:wide][:, lanes]
        keys = qkv[at, slot, :, wide : 2 * wide][:, lanes]
        values = qkv[at, slot, :, 2 * wide : 3 * wide][:, lanes]
        scores = dot(queries, keys, 1, 1) + bias[at, slot, head, span].astype(F32)
        powers = jnp.exp(scores - jnp.max(scores, -1, keepdims=True))
        weights = (powers / jnp.sum(powers, -1, keepdims=True)).astype(BF16)
        weights_kept[at, slot, head, span] = weights
        heads.append(dot(weights, values).astype(BF16))
    heads.append(jnp.zeros((rows, wide - head_count * HEAD_DIM), BF16))
    mixture[at, slot, span] = jnp.concatenate(heads, -1)


def forward_body(
    layer_count,
    head_count,
    tokens,
    w_qkv,
    qkv_bias,
    w_out,
    w_up,
    up_bias,
    w_down,
    bias,
    ln_gain,
    ln_bias,
    layer_scale,
    row_bias,
    gath_a_out,
    qkv_out,
    weights_out,
    mixture_out,
    gath_b_out,
    slope_out,
    active_out,
    normal_a,
    normal_b,
    inverse,
    branch_a,
    branch_b,
    stream,
    gath_a,
    qkv,
    weights_kept,
    mixture,
    gath_b,
    slope,
    active,
    hidden,
    part,
    got,
    summed,
    own,
    send_sems,
    recv_sems,
    out_sems,
):
    rows, width = stream.shape
    half = rows // PARTS
    group = Group(send_sems, recv_sems)
    group.meet()

    def each_chunk(body):
        step, count = by_chunk(rows, lambda span, carry: (body(span), carry)[1])
        lax.fori_loop(0, count, step, 0)

    def load(span):
        stream[span] = tokens[span].astype(F32)

    each_chunk(load)

    kept = (
        (gath_a, gath_a_out),
        (qkv, qkv_out),
        (weights_kept, weights_out),
        (mixture, mixture_out),
        (gath_b, gath_b_out),
        (slope, slope_out),
        (active, active_out),
    )

    def keep(number, at):
        source, target = kept[number]
        return pltpu.make_async_copy(source.at[at], target.at[at], out_sems.at[number, at])

    def layer(at, carry):
        trade = Exchange(group, 0, gath_a.at[at], part, got, summed)

        def enter(span):
            low, normal, inv = norm_chunk(
                stream[span], ln_gain[at, 0:1], ln_bias[at, 0:1]
            )
            gath_a[at, 0, span] = low
            normal_a[at, span] = normal
            inverse[at, 0, span] = jnp.broadcast_to(inv, (CHUNK, 128))

        each_chunk(enter)
        trade.start()
        scale = jnp.concatenate(
            [
                jnp.full((1, width // 3), HEAD_DIM**-0.5, F32),
                jnp.full((1, 2 * width // 3), 1.0, F32),
            ],
            -1,
        )

        def project(slot, first, count):
            span = pl.ds(first, count)
            mixed = dot(gath_a[at, slot, span], w_qkv[at])
            mixed = (mixed + qkv_bias[at]).astype(BF16).astype(F32) * scale
            qkv[at, slot, span] = mixed.astype(BF16)

        def attend(slot, first):
            attend_rows(qkv, weights_kept, mixture, bias, at, slot, first, head_count)

        def leave(slot, first):
            return dot(mixture[at, slot, pl.ds(first, half)], w_out[at])

        def whole(slot):
            project(slot, 0, rows)

            def one(place, carry):
                first = pl.multiple_of(place * half, half)
                attend(slot, first)
                result = leave(slot, first)
                if slot == 0:
                    own[pl.ds(first, half)] = result
                else:
                    part[slot, pl.ds(first, half)] = result.astype(BF16)
                return carry

            lax.fori_loop(0, PARTS, one, 0)

        whole(0)
        trade.to_near.wait_recv()
        whole(1)
        trade.sum_near.start()
        for place in range(PARTS):
            trade.pass_on(place)
            project(2, place * half, half)
        for place in range(PARTS):
            trade.relay[place].wait_recv()
            project(3, place * half, half)
        keep(0, at).start()
        keep(1, at).start()
        for place in range(PARTS):
            first = place * half
            attend(3, first)
            part[3, pl.ds(first, half)] = leave(3, first).astype(BF16)
            trade.sum_pair[place].start()
            attend(2, first)
            part[2, pl.ds(first, half)] = leave(2, first).astype(BF16)
            trade.send_sum(place)
        keep(2, at).start()
        keep(3, at).start()
        trade.finish()

        trade_b = Exchange(group, Exchange.COPIES, gath_b.at[at], part, got, summed)

        def between(span):
            total = own[span] + got[0, span].astype(F32) + got[2, span].astype(F32)
            branch = total + row_bias[at, 0:1]
            branch_a[at, span] = branch
            middle = stream[span] + layer_scale[at, 0:1] * branch
            stream[span] = middle
            low, normal, inv = norm_chunk(middle, ln_gain[at, 1:2], ln_bias[at, 1:2])
            gath_b[at, 0, span] = low
            normal_b[at, span] = normal
            inverse[at, 1, span] = jnp.broadcast_to(inv, (CHUNK, 128))

        each_chunk(between)
        trade.drain()

        trade_b.start()

        def raise_rows(values, count, put):
            hidden[pl.ds(0, count)] = dot(values, w_up[at]) + up_bias[at]

            def act(place, carry):
                span = pl.ds(pl.multiple_of(place * 16, 16), 16)
                high, incline = gelu_parts(hidden[span])
                put(place * 16, high.astype(BF16), incline.astype(BF16))
                return carry

            lax.fori_loop(0, count // 16, act, 0)

        def to_slot(slot, start):
            def put(first, high, incline):
                span = pl.ds(pl.multiple_of(start + first, 16), 16)
                active[at, slot, span] = high
                slope[at, slot, span] = incline

            return put

        raise_rows(gath_b[at, 0], rows, to_slot(0, 0))
        own[...] = dot(active[at, 0], w_down[at])
        trade_b.to_near.wait_recv()
        raise_rows(gath_b[at, 1], rows, to_slot(1, 0))
        part[1] = dot(active[at, 1], w_down[at]).astype(BF16)
        trade_b.sum_near.start()
        for place in range(PARTS):
            trade_b.pass_on(place)
            span = pl.ds(place * half, half)
            raise_rows(gath_b[at, 2, span], half, to_slot(2, place * half))
            trade_b.relay[place].wait_recv()
            raise_rows(gath_b[at, 3, span], half, to_slot(3, place * half))
            part[3, span] = dot(active[at, 3, span], w_down[at]).astype(BF16)
            trade_b.sum_pair[place].start()
            part[2, span] = dot(active[at, 2, span], w_down[at]).astype(BF16)
            trade_b.send_sum(place)
        for number in (4, 5, 6):
            keep(number, at).start()
        trade_b.finish()

        def after(span):
            total = own[span] + got[0, span].astype(F32) + got[2, span].astype(F32)
            branch = total + row_bias[at, 1:2]
            branch_b[at, span] = branch
            stream[span] = stream[span] + layer_scale[at, 1:2] * branch

        each_chunk(after)
        trade_b.drain()
        return carry

    lax.fori_loop(0, layer_count, layer, 0)
    for at in range(layer_count):
        for number in range(len(kept)):
            keep(number, at).wait()


def run_forward(tokens, weights, bias, norms, head_count):
    rows, width = tokens.shape
    w_qkv, qkv_bias, w_out, w_up, up_bias, w_down = weights
    layers = w_qkv.shape[0]
    wide = w_qkv.shape[2] // 3
    inner = w_up.shape[2]
    in_vmem = pl.BlockSpec(memory_space=pltpu.VMEM)
    in_hbm = pl.BlockSpec(memory_space=pl.ANY)
    kept = [
        jax.ShapeDtypeStruct((layers, 4) + tail, BF16)
        for tail in (
            (rows, width),
            (rows, 3 * wide),
            (head_count, rows, rows),
            (rows, wide),
            (rows, width),
            (rows, inner),
            (rows, inner),
        )
    ]
    near = [
        jax.ShapeDtypeStruct(shape, F32)
        for shape in (
            (layers, rows, width),
            (layers, rows, width),
            (layers, 2, rows, 128),
            (layers, rows, width),
            (layers, rows, width),
            (rows, width),
        )
    ]
    return pl.pallas_call(
        functools.partial(forward_body, layers, head_count),
        name="forward",
        out_shape=kept + near,
        in_specs=[in_vmem] * 12,
        out_specs=[in_hbm] * len(kept) + [in_vmem] * len(near),
        scratch_shapes=[pltpu.VMEM(leaf.shape, leaf.dtype) for leaf in kept]
        + [
            pltpu.VMEM((rows, inner), F32),
            pltpu.VMEM((4, rows, width), BF16),
            pltpu.VMEM((3, rows, width), BF16),
            pltpu.VMEM((rows, width), BF16),
            pltpu.VMEM((rows, width), F32),
            pltpu.SemaphoreType.DMA((2 * Exchange.COPIES,)),
            pltpu.SemaphoreType.DMA((2 * Exchange.COPIES,)),
            pltpu.SemaphoreType.DMA((len(kept), layers)),
        ],
        compiler_params=pltpu.CompilerParams(
            collective_id=0, has_side_effects=True, vmem_limit_bytes=64 * 1024 * 1000
        ),
    )(tokens, w_qkv, qkv_bias, w_out, w_up, up_bias, w_down, bias, *norms)


def fold(values):
    return jnp.sum(values.reshape(-1, 8, values.shape[-1]), 0)


def enter_back(grad, branch, scale, gath, sums):
    rows, width = grad.shape

    def body(span, carry):
        values = grad[span]
        gath[0, span] = (values * scale).astype(BF16)
        return carry[0] + fold(values * branch[span]), carry[1] + fold(values)

    step, count = by_chunk(rows, body)
    zero = jnp.zeros((8, width), F32)
    by_branch, alone = lax.fori_loop(0, count, step, (zero, zero))
    sums[2:3] = jnp.sum(by_branch, 0, keepdims=True)
    sums[3:4] = jnp.sum(alone, 0, keepdims=True) * scale


def leave_back(grad, own, got, normal, inverse, gain, grad_out, sums):
    rows, width = grad.shape

    def body(span, carry):
        total = own[span] + got[0, span].astype(F32) + got[2, span].astype(F32)
        unit = normal[span]
        scaled = total * gain
        centered = (
            scaled
            - jnp.mean(scaled, -1, keepdims=True)
            - unit * jnp.mean(scaled * unit, -1, keepdims=True)
        )
        grad_out[span] = grad[span] + inverse[span, 0:1] * centered
        return carry[0] + fold(total * unit), carry[1] + fold(total)

    step, count = by_chunk(rows, body)
    zero = jnp.zeros((8, width), F32)
    by_unit, alone = lax.fori_loop(0, count, step, (zero, zero))
    sums[0:1] = jnp.sum(by_unit, 0, keepdims=True)
    sums[1:2] = jnp.sum(alone, 0, keepdims=True)


def weight_grad(left, right, out):
    block = 256

    def step(place, carry):
        span = pl.ds(pl.multiple_of(place * block, block), block)
        total = None
        for slot in range(4):
            term = dot(left[slot, :, span], right[slot], 0, 0)
            total = term if total is None else total + term
        out[span] = total.astype(out.dtype)
        return carry

    lax.fori_loop(0, out.shape[0] // block, step, 0)


class Loads:
    def __init__(self, sems):
        self.sems = sems
        self.steps = []

    def add(self, source, target):
        step = pltpu.make_async_copy(source, target, self.sems.at[len(self.steps)])
        step.start()
        self.steps.append(step)
        return len(self.steps) - 1

    def ready(self, *numbers):
        for number in numbers:
            self.steps[number].wait()


def back_mlp_body(
    at,
    grad,
    branch_all,
    normal_all,
    inverse_all,
    active_all,
    slope_all,
    gath_b_all,
    w_up_all,
    w_down_all,
    ln_gain,
    layer_scale,
    grad_out,
    d_up,
    d_down,
    sums,
    d_up_bias,
    branch,
    normal,
    inverse,
    active,
    slope,
    gath_b,
    w_up,
    w_down,
    gath,
    d_hidden,
    hidden,
    part,
    got,
    summed,
    own,
    send_sems,
    recv_sems,
    load_sems,
):
    rows = grad.shape[0]
    half = rows // PARTS
    loads = Loads(load_sems)
    loads.add(branch_all.at[at], branch)
    loads.add(w_down_all.at[at], w_down)
    loads.add(slope_all.at[at], slope)
    loads.add(w_up_all.at[at], w_up)
    loads.add(normal_all.at[at], normal)
    loads.add(inverse_all.at[at, 1], inverse)
    loads.add(active_all.at[at], active)
    loads.add(gath_b_all.at[at], gath_b)
    group = Group(send_sems, recv_sems)
    group.meet()
    trade = Exchange(group, 0, gath, part, got, summed)
    loads.ready(0)
    enter_back(grad, branch, layer_scale[at, 1:2], gath, sums)
    trade.start()
    loads.ready(1, 2, 3)

    def down(slot, first, count, total):
        span = pl.ds(first, count)
        hidden[pl.ds(0, count)] = dot(gath[slot, span], w_down[...], 1, 1)

        def body(place, carry):
            inside = pl.ds(pl.multiple_of(place * CHUNK, CHUNK), CHUNK)
            there = pl.ds(pl.multiple_of(first + place * CHUNK, CHUNK), CHUNK)
            low = (hidden[inside] * slope[slot, there].astype(F32)).astype(BF16)
            d_hidden[slot, there] = low
            return carry + fold(low.astype(F32))

        return lax.fori_loop(0, count // CHUNK, body, total)

    def back(slot, first, count):
        return dot(d_hidden[slot, pl.ds(first, count)], w_up[...], 1, 1)

    total = jnp.zeros((8, d_up_bias.shape[1]), F32)
    total = down(0, 0, rows, total)
    own[...] = back(0, 0, rows)
    trade.to_near.wait_recv()
    total = down(1, 0, rows, total)
    part[1] = back(1, 0, rows).astype(BF16)
    trade.sum_near.start()
    for place in range(PARTS):
        trade.pass_on(place)
        first = place * half
        span = pl.ds(first, half)
        total = down(2, first, half, total)
        trade.relay[place].wait_recv()
        total = down(3, first, half, total)
        part[3, span] = back(3, first, half).astype(BF16)
        trade.sum_pair[place].start()
        part[2, span] = back(2, first, half).astype(BF16)
        trade.send_sum(place)
    d_up_bias[...] = jnp.sum(total, 0, keepdims=True)
    loads.ready(4, 5, 6, 7)
    weight_grad(active, gath, d_down)
    weight_grad(gath_b, d_hidden, d_up)
    trade.finish()
    leave_back(grad, own, got, normal, inverse, ln_gain[at, 1:2], grad_out, sums)
    trade.drain()


def run_back_mlp(at, grad, kept, weights, norms):
    rows, width = grad.shape
    branch, normal, inverse, active, slope, gath_b = kept
    w_up, w_down = weights
    inner = w_up.shape[2]
    in_vmem = pl.BlockSpec(memory_space=pltpu.VMEM)
    in_hbm = pl.BlockSpec(memory_space=pl.ANY)
    own_rows = pltpu.VMEM((rows, width), F32)
    four = pltpu.VMEM((4, rows, width), BF16)
    four_inner = pltpu.VMEM((4, rows, inner), BF16)
    return pl.pallas_call(
        functools.partial(back_mlp_body, at),
        name="back_mlp",
        out_shape=[
            jax.ShapeDtypeStruct((rows, width), F32),
            jax.ShapeDtypeStruct((width, inner), BF16),
            jax.ShapeDtypeStruct((inner, width), BF16),
            jax.ShapeDtypeStruct((8, width), F32),
            jax.ShapeDtypeStruct((1, inner), F32),
        ],
        in_specs=[in_vmem] + [in_hbm] * 8 + [in_vmem] * 2,
        out_specs=[in_vmem] * 5,
        scratch_shapes=[
            own_rows,
            own_rows,
            pltpu.VMEM((rows, 128), F32),
            four_inner,
            four_inner,
            four,
            pltpu.VMEM((width, inner), BF16),
            pltpu.VMEM((inner, width), BF16),
            four,
            four_inner,
            pltpu.VMEM((rows, inner), F32),
            four,
            pltpu.VMEM((3, rows, width), BF16),
            pltpu.VMEM((rows, width), BF16),
            own_rows,
            pltpu.SemaphoreType.DMA((Exchange.COPIES,)),
            pltpu.SemaphoreType.DMA((Exchange.COPIES,)),
            pltpu.SemaphoreType.DMA((8,)),
        ],
        compiler_params=pltpu.CompilerParams(
            collective_id=1 + 2 * at, has_side_effects=True, vmem_limit_bytes=48 * 1024 * 1000
        ),
    )(grad, branch, normal, inverse, active, slope, gath_b, w_up, w_down, norms[0], norms[2])


def back_attend_body(
    at,
    head_count,
    grad,
    branch_all,
    normal_all,
    inverse_all,
    mixture_all,
    qkv_all,
    weights_all,
    gath_a_all,
    w_out_all,
    w_qkv_all,
    spots,
    ln_gain,
    layer_scale,
    grad_out,
    d_qkv,
    d_out,
    sums,
    d_qkv_bias,
    d_grid,
    branch,
    normal,
    inverse,
    mixture,
    qkv,
    weights,
    gath_a,
    w_out,
    w_qkv,
    gath,
    d_mixed,
    d_scores,
    part,
    got,
    summed,
    own,
    send_sems,
    recv_sems,
    load_sems,
):
    rows = grad.shape[0]
    half = rows // PARTS
    wide = mixture.shape[2]
    loads = Loads(load_sems)
    loads.add(branch_all.at[at], branch)
    loads.add(w_out_all.at[at], w_out)
    loads.add(qkv_all.at[at], qkv)
    loads.add(weights_all.at[at], weights)
    loads.add(w_qkv_all.at[at], w_qkv)
    loads.add(normal_all.at[at], normal)
    loads.add(inverse_all.at[at, 0], inverse)
    loads.add(mixture_all.at[at], mixture)
    loads.add(gath_a_all.at[at], gath_a)
    group = Group(send_sems, recv_sems)
    group.meet()
    trade = Exchange(group, 0, gath, part, got, summed)
    loads.ready(0)
    enter_back(grad, branch, layer_scale[at, 0:1], gath, sums)
    trade.start()
    loads.ready(1, 2, 3, 4)
    spare = jnp.zeros((rows, wide - head_count * HEAD_DIM), BF16)

    def attend(slot):
        d_mix = dot(gath[slot], w_out[...], 1, 1).astype(BF16)
        pieces = ([], [], [])
        for head in range(head_count):
            lanes = slice(head * HEAD_DIM, (head + 1) * HEAD_DIM)
            queries = qkv[slot, :, 0:wide][:, lanes]
            keys = qkv[slot, :, wide : 2 * wide][:, lanes]
            values = qkv[slot, :, 2 * wide : 3 * wide][:, lanes]
            share = weights[slot, head]
            d_head = d_mix[:, lanes]
            wide_share = share.astype(F32)
            d_share = dot(d_head, values, 1, 1)
            middle = jnp.sum(wide_share * d_share, -1, keepdims=True)
            d_score = (wide_share * (d_share - middle)).astype(BF16)
            d_scores[slot, head] = d_score
            pieces[0].append((dot(d_score, keys) * HEAD_DIM**-0.5).astype(BF16))
            pieces[1].append(dot(d_score, queries, 0, 0).astype(BF16))
            pieces[2].append(dot(share, d_head, 0, 0).astype(BF16))
        for place in range(3):
            d_mixed[slot, :, place * wide : (place + 1) * wide] = jnp.concatenate(
                pieces[place] + [spare], -1
            )

    def back(slot, first, count):
        return dot(d_mixed[slot, pl.ds(first, count)], w_qkv[...], 1, 1)

    attend(0)
    own[...] = back(0, 0, rows)
    trade.to_near.wait_recv()
    attend(1)
    part[1] = back(1, 0, rows).astype(BF16)
    trade.sum_near.start()
    for place in range(PARTS):
        trade.pass_on(place)
    for place in range(PARTS):
        trade.relay[place].wait_recv()
    attend(3)
    part[3] = back(3, 0, rows).astype(BF16)
    for place in range(PARTS):
        trade.sum_pair[place].start()
    attend(2)
    for place in range(PARTS):
        first = place * half
        part[2, pl.ds(first, half)] = back(2, first, half).astype(BF16)
        trade.send_sum(place)
    loads.ready(5, 6, 7, 8)

    def add(slot, total):
        def body(span, carry):
            return carry + fold(d_mixed[slot, span].astype(F32))

        step, count = by_chunk(rows, body)
        return lax.fori_loop(0, count, step, total)

    total = jnp.zeros((8, 3 * wide), F32)
    for slot in range(4):
        total = add(slot, total)
    d_qkv_bias[...] = jnp.sum(total, 0, keepdims=True)
    weight_grad(gath_a, d_mixed, d_qkv)
    weight_grad(mixture, gath, d_out)
    for head in range(head_count):
        total = None
        for slot in range(4):
            placed = dot(spots[slot], d_scores[slot, head], 0, 0).astype(BF16)
            term = dot(placed, spots[slot])
            total = term if total is None else total + term
        d_grid[head] = total
    trade.finish()
    leave_back(grad, own, got, normal, inverse, ln_gain[at, 0:1], grad_out, sums)
    trade.drain()


def run_back_attend(at, grad, kept, weights, spots, norms):
    rows, width = grad.shape
    branch, normal, inverse, mixture, qkv, shares, gath_a = kept
    w_out, w_qkv = weights
    wide = w_out.shape[1]
    head_count = shares.shape[2]
    in_vmem = pl.BlockSpec(memory_space=pltpu.VMEM)
    in_hbm = pl.BlockSpec(memory_space=pl.ANY)
    own_rows = pltpu.VMEM((rows, width), F32)
    four = pltpu.VMEM((4, rows, width), BF16)
    mixed = pltpu.VMEM((4, rows, 3 * wide), BF16)
    square = pltpu.VMEM((4, head_count, rows, rows), BF16)
    return pl.pallas_call(
        functools.partial(back_attend_body, at, head_count),
        name="back_attend",
        out_shape=[
            jax.ShapeDtypeStruct((rows, width), F32),
            jax.ShapeDtypeStruct((width, 3 * wide), BF16),
            jax.ShapeDtypeStruct((wide, width), BF16),
            jax.ShapeDtypeStruct((8, width), F32),
            jax.ShapeDtypeStruct((1, 3 * wide), F32),
            jax.ShapeDtypeStruct((head_count, rows, rows), F32),
        ],
        in_specs=[in_vmem] + [in_hbm] * 9 + [in_vmem] * 3,
        out_specs=[in_vmem] * 6,
        scratch_shapes=[
            own_rows,
            own_rows,
            pltpu.VMEM((rows, 128), F32),
            pltpu.VMEM((4, rows, wide), BF16),
            mixed,
            square,
            four,
            pltpu.VMEM((wide, width), BF16),
            pltpu.VMEM((width, 3 * wide), BF16),
            four,
            mixed,
            square,
            four,
            pltpu.VMEM((3, rows, width), BF16),
            pltpu.VMEM((rows, width), BF16),
            own_rows,
            pltpu.SemaphoreType.DMA((Exchange.COPIES,)),
            pltpu.SemaphoreType.DMA((Exchange.COPIES,)),
            pltpu.SemaphoreType.DMA((9,)),
        ],
        compiler_params=pltpu.CompilerParams(
            collective_id=2 + 2 * at, has_side_effects=True, vmem_limit_bytes=48 * 1024 * 1000
        ),
    )(
        grad,
        branch,
        normal,
        inverse,
        mixture,
        qkv,
        shares,
        gath_a,
        w_out,
        w_qkv,
        spots,
        norms[0],
        norms[2],
    )


def place_rows(index_rows, lengths, bin_rows):
    bin_total = lengths.shape[0]
    index_bins = index_rows.reshape(bin_total, bin_rows, bin_rows)
    first, both = lengths[:, 0:1], lengths[:, 0:1] + lengths[:, 1:2]
    code_first = index_bins[:, 1]
    code_second = jnp.concatenate(
        [
            lax.dynamic_slice(index_bins, (at, lengths[at, 0] + 1, 0), (1, 1, bin_rows))[0]
            for at in range(bin_total)
        ]
    )
    at = jnp.arange(bin_rows)[None]
    code = (SIDE - 1) * (STRIDE + 1) - jnp.where(at < first, code_first, code_second)
    cell = (code // STRIDE) * SIDE + code % STRIDE
    cell = jnp.where((at == 0) | (at == first), CELLS, cell)
    cell = jnp.where(at < both, cell, bin_rows - 1)
    return (cell[:, :, None] == jnp.arange(bin_rows)[None, None]).astype(BF16)


def grid_table(table_used, bin_rows):
    layer_count, entries, head_count = table_used.shape
    columns = jnp.transpose(table_used, (0, 2, 1)).reshape(layer_count * head_count, entries)
    turned = columns[:, STRIDE * STRIDE - 1 :: -1].reshape(-1, STRIDE, STRIDE)
    by_col = jnp.stack([turned[:, :, SIDE - 1 - c : STRIDE - c] for c in range(SIDE)], 1)
    by_row = jnp.stack([by_col[:, :, SIDE - 1 - r : STRIDE - r] for r in range(SIDE)], 1)
    grid = by_row.reshape(-1, CELLS, CELLS)
    grid = jnp.pad(grid, ((0, 0), (0, bin_rows - CELLS), (0, bin_rows - CELLS)))
    row = lax.broadcasted_iota(jnp.int32, (1, bin_rows, bin_rows), 1)
    col = lax.broadcasted_iota(jnp.int32, (1, bin_rows, bin_rows), 2)
    last = columns[:, STRIDE * STRIDE :, None, None]
    grid = jnp.where((row == CELLS) & (col < CELLS), last[:, 0], grid)
    grid = jnp.where((col == CELLS) & (row < CELLS), last[:, 1], grid)
    grid = jnp.where((row == CELLS) & (col == CELLS), last[:, 2], grid)
    return grid.reshape(layer_count, head_count, bin_rows, bin_rows)


def look_up(spots, grid, same_image):
    half = jnp.einsum("bip,lhpq->lbhiq", spots, grid)
    looked = jnp.einsum("lbhiq,bjq->lbhij", half, spots)
    return jnp.where(same_image[None, :, None], looked, jnp.asarray(-1000000000.0, BF16))


def skew(values):
    flipped = values[..., ::-1, :]
    padded = jnp.pad(flipped, [(0, 0)] * (values.ndim - 1) + [(0, SIDE)])
    flat = padded.reshape(padded.shape[:-2] + (SIDE * 2 * SIDE,))[..., : SIDE * STRIDE]
    return jnp.sum(flat.reshape(padded.shape[:-2] + (SIDE, STRIDE)), -2)


def table_grad(total):
    layer_count, head_count = total.shape[:2]
    cells = total[:, :, :CELLS, :CELLS].reshape(-1, SIDE, SIDE, SIDE, SIDE)
    by_col = skew(jnp.transpose(cells, (0, 1, 3, 2, 4)))
    by_both = skew(jnp.transpose(by_col, (0, 3, 1, 2)))
    offsets = jnp.transpose(by_both, (0, 2, 1)).reshape(-1, STRIDE * STRIDE)[:, ::-1]
    offsets = offsets.reshape(layer_count, head_count, -1)
    tail = jnp.stack(
        [
            jnp.sum(total[:, :, CELLS, :CELLS], -1),
            jnp.sum(total[:, :, :CELLS, CELLS], -1),
            total[:, :, CELLS, CELLS],
        ],
        -1,
    )
    return jnp.transpose(jnp.concatenate([offsets, tail], -1), (0, 2, 1))


def per_device(
    tokens,
    cotangent,
    segments,
    lengths,
    rel_index,
    w_qkv,
    qv_bias,
    w_out,
    w_fc1,
    fc1_bias,
    w_fc2,
    rel_table,
    ln_gain,
    ln_bias,
    layer_scale,
    row_bias,
):
    own_rows, width = tokens.shape
    group_rows, bin_rows = rel_index.shape
    layer_count = w_qkv.shape[0]
    head_count = rel_table.shape[2]
    local_width = w_qkv.shape[3]
    wide = -(-local_width // 256) * 256
    bin_total = group_rows // bin_rows
    place = lax.axis_index("tensor")
    assert own_rows == bin_rows and bin_total == 4

    order = jnp.stack([place, place + 1 - 2 * (place % 2), (place + 2) % 4, 3 - place])
    own_length = jnp.sum(lax.dynamic_slice_in_dim(lengths, place, 1))
    valid = (jnp.arange(own_rows) < own_length)[:, None]
    seg_bins = jnp.take(segments.reshape(bin_total, bin_rows), order, axis=0)
    same_image = seg_bins[:, :, None] == seg_bins[:, None, :]
    spots = jnp.take(place_rows(rel_index, lengths, bin_rows), order, axis=0)
    bias = look_up(spots, grid_table(rel_table, bin_rows), same_image)

    extra = wide - local_width
    qkv_used = jnp.pad(w_qkv, ((0, 0), (0, 0), (0, 0), (0, extra))).reshape(
        layer_count, width, 3 * wide
    )
    out_used = jnp.pad(w_out, ((0, 0), (0, extra), (0, 0)))
    zero_bias = jnp.zeros((layer_count, wide), F32)
    qv = jnp.pad(qv_bias.astype(F32), ((0, 0), (0, 0), (0, extra)))
    qkv_bias = jnp.concatenate([qv[:, 0], zero_bias, qv[:, 1]], -1)[:, None]
    up_bias = fc1_bias.astype(F32)[:, None]
    norms = (ln_gain, ln_bias, layer_scale, row_bias)

    (
        gath_a,
        qkv,
        shares,
        mixture,
        gath_b,
        slope,
        active,
        normal_a,
        normal_b,
        inverse,
        branch_a,
        branch_b,
        stream,
    ) = run_forward(
        tokens, (qkv_used, qkv_bias, out_used, w_fc1, up_bias, w_fc2), bias, norms, head_count
    )
    result = jnp.where(valid, stream, 0.0).astype(BF16)
    gradient = jnp.where(valid, cotangent.astype(F32), 0.0)

    weight_parts = [None] * layer_count
    row_parts = [None] * layer_count
    up_biases = [None] * layer_count
    qkv_biases = [None] * layer_count
    grids = [None] * layer_count
    for at in reversed(range(layer_count)):
        gradient, d_up, d_down, sums_b, up_biases[at] = run_back_mlp(
            at, gradient, (branch_b, normal_b, inverse, active, slope, gath_b), (w_fc1, w_fc2), norms
        )
        d_up, d_down = lax.psum((d_up, d_down), "dp")
        gradient, d_qkv, d_out, sums_a, qkv_biases[at], grids[at] = run_back_attend(
            at,
            gradient,
            (branch_a, normal_a, inverse, mixture, qkv, shares, gath_a),
            (out_used, qkv_used),
            spots,
            norms,
        )
        d_qkv, d_out = lax.psum((d_qkv, d_out), "dp")
        weight_parts[at] = (d_qkv, d_out, d_up, d_down)
        row_parts[at] = jnp.stack([sums_a[:4], sums_b[:4]], 1)
    d_qkv, d_out, d_up, d_down = [
        jnp.stack(parts).astype(F32) for parts in zip(*weight_parts)
    ]
    d_qkv = d_qkv.reshape(layer_count, width, 3, wide)[..., :local_width]
    d_out = d_out[:, :local_width]
    d_bias = jnp.concatenate(qkv_biases).reshape(layer_count, 3, wide)[:, ::2, :local_width]
    d_table = table_grad(jnp.stack(grids))
    d_bias, d_up_bias, d_table = lax.psum((d_bias, jnp.concatenate(up_biases), d_table), "dp")
    rows_all = lax.psum(jnp.stack(row_parts, 1), ("dp", "tensor"))
    return (
        result,
        gradient,
        d_qkv,
        d_bias,
        d_out,
        d_up,
        d_up_bias,
        d_down,
        d_table,
        rows_all[0],
        rows_all[1],
        rows_all[2],
        rows_all[3],
    )


def solution(mesh):
    in_specs = (
        P(("dp", "tensor"), None),
        P(("dp", "tensor"), None),
        P("dp"),
        P("dp", None),
        P("dp", None),
        P(None, None, None, "tensor"),
        P(None, None, "tensor"),
        P(None, "tensor", None),
        P(None, None, "tensor"),
        P(None, "tensor"),
        P(None, "tensor", None),
        P(None, None, "tensor"),
        P(),
        P(),
        P(),
        P(),
    )
    out_specs = (
        P(("dp", "tensor"), None),
        P(("dp", "tensor"), None),
        P(None, None, None, "tensor"),
        P(None, None, "tensor"),
        P(None, "tensor", None),
        P(None, None, "tensor"),
        P(None, "tensor"),
        P(None, "tensor", None),
        P(None, None, "tensor"),
        P(),
        P(),
        P(),
        P(),
    )
    return jax.shard_map(
        per_device, mesh=mesh, in_specs=in_specs, out_specs=out_specs, check_vma=False
    )
```

time: 840 us -> 572 us (0.68)
  waiting for transfers between devices: 388 us -> 117 us
  Pallas kernels: 0 us -> 208 us
  matrix products: 105 us -> 4.11 us
  other arithmetic: 83.4 us -> 24 us
  local copies, waits for them, and re-layouts: 156 us -> 108 us
    pallas_call x0 -> x5, Pallas kernels: none -> 208 us  [the longest x1 106 us: run_forward(): pl.pallas_call(functools.partial(forward_body, layers, head_count), name=...]
    reduce_scatter x8 -> x0, waiting for transfers between devices: 193 us -> none  [the longest x4 113 us: project_rows(): lax.psum_scatter(jnp.dot(left_side, right_side, preferred_element_type=jn...]
    all_gather x8 -> x0, waiting for transfers between devices: 115 us -> none  [the longest x4 65.1 us: spread_grads(): return lax.all_gather(values, 'tensor', axis=0, tiled=True)]
    dot_general x38 -> x1, matrix products: 104 us -> 3.06 us  [look_up(): looked = jnp.einsum('lbhiq,bjq->lbhij', half, spots)]
    psum x1, waiting for transfers between devices: 80.1 us -> 117 us  [per_device(): d_qkv, d_out = lax.psum((d_qkv, d_out), 'dp')]
    reduce_sum x18 -> x1, other arithmetic: 27.3 us -> 1.39 us  [per_device(): own_length = jnp.sum(lax.dynamic_slice_in_dim(lengths, place, 1))]
    convert_element_type x15 -> x4, other arithmetic: 24.6 us -> 6.05 us  [the longest x2 4.98 us: per_device(): jnp.stack(parts).astype(F32)]
    convert_element_type x16 -> x0, local copies, waits for them, and re-layouts: 16.6 us -> none  [the longest x4 4.64 us: attend_back(): grad_key.reshape(flat_shape).astype(jnp.bfloat16)]
  transfers between devices with their start and end apart: 17 -> 1, of which waited for: 15 -> 1; matrix products, arithmetic and copies ran while one was open for 21% -> 11% of each run, Pallas kernels for 0% -> 0%
where the time goes in v2:
time: 572 us; the launch traced here: 565 us
  Pallas kernels  208 us (36%)
  waiting for transfers between devices  117 us (20%)
  local copies, waits for them, and re-layouts  108 us (19%)
  blocking collectives  83.2 us (15%)
  other arithmetic  24 us (4%)
  between operations  20.4 us (4%)
    psum x1, waiting for transfers between devices, per_device(): d_qkv, d_out = lax.psum((d_qkv, d_out), 'dp')  117 us
    pallas_call x1, Pallas kernels, run_forward(): pl.pallas_call(functools.partial(forward_body, layers, head_count), name=...  106 us
    pallas_call x2, Pallas kernels, run_back_attend(): pl.pallas_call(functools.partial(back_attend_body, at, head_count), name=...  55.9 us
    pallas_call x2, Pallas kernels, run_back_mlp(): pl.pallas_call(functools.partial(back_mlp_body, at), name='back_mlp', out...  46.8 us
    psum x1, blocking collectives, per_device(): rows_all = lax.psum(jnp.stack(row_parts, 1), ('dp', 'tensor'))  43.7 us
    unnamed x136, local copies, waits for them, and re-layouts  40 us
    psum x1, blocking collectives, per_device(): lax.psum((d_bias, jnp.concatenate(up_biases), d_table), 'dp')  39.5 us
  transfers between devices with their start and end apart: 1, of which 1 were waited for; matrix products, arithmetic and copies ran while one was open for 11% of the time, Pallas kernels for 0%

profile of v2, /device:TPU:0, one launch (start us, length us, event | category | flops | bytes accessed | tf_op | source)
XLA Modules:
  0.0 564.7 jit_solution(2671503315167723051)
XLA Ops:
  8.0 1.4 fusion.41
  14.6 1.4 fusion.34
  19.6 1.3 reshape.534.up_bias
  28.2 1.6 pad.27
  29.7 4.3 copy.59.w_qkv.w_qkv_all
  46.0 6.6 %reshape.553 = bf16[6,196,196]{2,0,1:T(8,128)(2,1)S(1)} reshape(bf16[6,14,14,14,14]{4,3,0,2,1:T(8,128)(2,1)} %fusion.12) | data formatting | bytes 921984 | tf_op jit(solution)/shard_map/reshape | solution.py:879
  53.5 1.0 convolution_bitcast_fusion
  54.6 3.1 bitcast_select_fusion.bias
  57.6 105.6 %forward.1 = (bf16[2,4,256,768]{3,2,1,0:T(8,128)(2,1)}, bf16[2,4,256,768]{3,2,1,0:T(8,128)(2,1)}, bf16[2,4,3,256,256]{4,3,2,1,0:T(8,128)(2,1)}, bf16[2,4,256,256...) custom-call(bf16[256,768]{1,0:T(8,128)(2,1)} %tokens.1, ...), custom_call_target="tpu_custom_call" | custom-call | tf_op jit(solution)/shard_map/forward/pallas_call | solution.py:410
  164.3 1.4 copy-done.2
  165.7 23.3 %back_mlp.2 = (f32[256,768]{1,0:T(8,128)S(1)}, bf16[768,768]{1,0:T(8,128)(2,1)S(1)}, bf16[768,768]{1,0:T(8,128)(2,1)S(1)}, f32[8,768]{1,0:T(8,128)S(1)}, f32[1,768]{1,0:T(1,128)S(1)}) custom-call(f32[256,768]{1,0:T(8,128)S(1)} %convert_select_fusion.grad, f32[2,256,768]{2,1,0:T(8,128)S(1)} %copy-done.2, f32[2,256,768]{2,1,0:T(8,128)} %get-tuple-element.50.normal_all, ...), custom_call_target="tpu_custom_call" | custom-call | tf_op jit(solution)/shard_map/back_mlp/pallas_call | solution.py:614
  191.1 28.0 %back_attend.2 = (f32[256,768]{1,0:T(8,128)S(1)}, bf16[768,768]{1,0:T(8,128)(2,1)S(1)}, bf16[256,768]{1,0:T(8,128)(2,1)S(1)}, f32[8,768]{1,0:T(8,128)S(1)}, f32[...) custom-call(f32[256,768]{1,0:T(8,128)S(1)} %get-tuple-element.55.grad, f32[2,256,768]{2,1,0:T(8,128)} %get-tuple-element.56.branch_all, ...), custom_call_target="tpu_custom_call" | custom-call | tf_op jit(solution)/shard_map/back_attend/pallas_call | solution.py:800
  221.4 23.5 %back_mlp.3 = (f32[256,768]{1,0:T(8,128)S(1)}, bf16[768,768]{1,0:T(8,128)(2,1)S(1)}, bf16[768,768]{1,0:T(8,128)(2,1)S(1)}, f32[8,768]{1,0:T(8,128)S(1)}, f32[1,768]{1,0:T(1,128)S(1)}) custom-call(f32[256,768]{1,0:T(8,128)S(1)} %get-tuple-element.62.grad, f32[2,256,768]{2,1,0:T(8,128)S(1)} %copy-done.3, f32[2,256,768]{2,1,0:T(8,128)} %get-tuple-element.50.normal_all, ...), custom_call_target="tpu_custom_call" | custom-call | tf_op jit(solution)/shard_map/back_mlp/pallas_call | solution.py:614
  248.2 27.9 %back_attend.3 = (f32[256,768]{1,0:T(8,128)S(1)}, bf16[768,768]{1,0:T(8,128)(2,1)S(1)}, bf16[256,768]{1,0:T(8,128)(2,1)S(1)}, f32[8,768]{1,0:T(8,128)S(1)}, f32[...) custom-call(f32[256,768]{1,0:T(8,128)S(1)} %get-tuple-element.63.grad, f32[2,256,768]{2,1,0:T(8,128)} %get-tuple-element.56.branch_all, ...), custom_call_target="tpu_custom_call" | custom-call | tf_op jit(solution)/shard_map/back_attend/pallas_call | solution.py:800
  279.0 2.5 copy.62
  281.5 1.6 copy.63
  286.5 43.7 %psum.95 = f32[4,2,2,768]{3,0,2,1:T(4,128)S(1)} all-reduce(f32[4,2,2,768]{3,0,2,1:T(4,128)S(1)} %pad_maximum_fusion.2), channel_id=1, replica_groups=mesh['dp'=8,'tensor'=4] {'dp','tensor'}, use_global_device_ids=true, to_apply=%region_16.17 | all-reduce | flops 12288 | bytes 98304 | tf_op jit(solution)/shard_map/psum | solution.py:1017
  332.7 1.1 fusion.5
  333.8 7.7 %reshape.527 = f32[6,14,14,14,14]{4,3,2,1,0:T(8,128)} reshape(f32[2,3,196,196]{3,2,1,0:T(8,128)} %fusion.5) | data formatting | bytes 1843968 | tf_op jit(solution)/shard_map/reshape | solution.py:905
  341.5 8.4 %rev.13 = f32[6,14,14,14,14]{4,2,3,1,0:T(8,128)} reverse(f32[6,14,14,14,14]{4,2,3,1,0:T(8,128)} %bitcast.242), dimensions={3} | reverse | bytes 1843968 | tf_op jit(solution)/shard_map/rev | solution.py:897
  350.0 7.7 %copy.87 = f32[6,14,14,14,14]{4,3,2,1,0:T(8,128)S(1)} copy(f32[6,14,14,14,14]{4,2,3,1,0:T(8,128)} %rev.13) | data formatting | bytes 1843968
  357.7 4.7 pad.32.clone
  362.4 7.2 %reshape.528 = f32[6,14,14,392]{3,2,1,0:T(8,128)S(1)} reshape(f32[6,14,14,14,28]{4,3,2,1,0:T(8,128)} %pad.32.clone) | data formatting | bytes 3687936 | tf_op jit(solution)/shard_map/reshape | solution.py:899
  369.6 1.6 slice.287
  371.1 8.5 %reshape.529 = f32[6,14,14,14,27]{4,3,2,1,0:T(8,128)} reshape(f32[6,14,14,378]{3,2,1,0:T(8,128)} %slice.287) | data formatting | bytes 3556224 | tf_op jit(solution)/shard_map/reshape | solution.py:900
  379.6 6.2 %reduce_sum.46 = f32[6,14,14,27]{3,2,1,0:T(8,128)S(1)} reduce(f32[6,14,14,14,27]{4,3,2,1,0:T(8,128)} %reshape.529, f32[]{:T(128)} %constant.93.clone.1), dimensions={3}, to_apply=%region_11.12 | reduce | flops 412776 | bytes 1905124 | tf_op jit(solution)/shard_map/reduce_sum | solution.py:900
  388.7 39.5 %all-reduce.6 = (f32[2,2,192]{2,1,0:T(2,128)}, f32[2,768]{1,0:T(2,128)}, f32[2,732,3]{1,2,0:T(4,128)S(1)}) all-reduce(f32[2,2,192]{2,1,0:T(2,128)S(1)} %copy-done.42, f32[2,768]{1,0:T(2,128)S(1)} %pad_maximum_fusion.5, f32[2,732,3]{1,2,0:T(4,128)S(1)} %maximum_bitcast_fusion), channel_id=1, replica_groups=mesh['dp'=8,'tensor'=4] {'dp'}, use_global_device_ids=true, to_apply=%region_3.4 | all-reduce | flops 6696 | bytes 53568 | tf_op jit(solution)/shard_map/psum | solution.py:1016
  429.6 117.0 %all-reduce.10.cloned.1.call-done = (bf16[1,768,3,256]{1,3,2,0:T(8,128)(2,1)}, bf16[1,768,3,256]{1,3,2,0:T(8,128)(2,1)}, bf16[1,256,768]{2,1,0:T(8,128)(2,1)}, b...) async-done(((bf16[1,768,3,256]{1,3,2,0:T(8,128)(2,1)}, ...) | async-done | bytes 7864336 | tf_op jit(solution)/shard_map/psum | solution.py:1006
  546.7 3.7 fusion.2
  550.4 1.1 fusion.9
  551.5 2.5 maximum_convert_fusion
  554.1 2.5 maximum_convert_fusion.1
  (200 shorter events, 46.7 us)
Async XLA Ops:
  7.2 20.0 %copy-start.37 = (bf16[2,192,768]{2,1,0:T(8,128)(2,1)S(1)}, bf16[2,192,768]{2,1,0:T(8,128)(2,1)}, u32[]{:S(2)}) copy-start(bf16[2,192,768]{2,1,0:T(8,128)(2,1)} %param.23) | copy-start | bytes 1769476
  7.2 539.5 %all-reduce.10.cloned.1.call-start = ((), (), s32[]{:S(2)}) async-start(), calls=%async_computation | async-start | bytes 15728640 | tf_op jit(solution)/shard_map/psum | solution.py:1006
  16.7 36.2 %copy-start.46 = (pred[256]{0:T(512)(128)(4,1)}, pred[256]{0:T(512)(128)(4,1)S(1)}, u32[]{:S(2)}) copy-start(pred[256]{0:T(512)(128)(4,1)S(1)} %iota_compare_fusion.7) | copy-start | bytes 772
  25.8 2.3 copy-start.31
  46.0 7.0 %copy-start.38 = (bf16[256,768]{1,0:T(8,128)(2,1)S(1)}, bf16[256,768]{1,0:T(8,128)(2,1)}, u32[]{:S(2)}) copy-start(bf16[256,768]{1,0:T(8,128)(2,1)} %param.17) | copy-start | bytes 1179652
  57.6 105.6 %copy-start.14 = (f32[2,2,768]{2,1,0:T(2,128)S(1)}, f32[2,2,768]{2,1,0:T(2,128)}, u32[]{:S(2)}) copy-start(f32[2,2,768]{2,1,0:T(2,128)} %ln_gain.9) | copy-start | bytes 36868
  57.6 105.6 %copy-start.15 = (f32[2,2,768]{2,1,0:T(2,128)S(1)}, f32[2,2,768]{2,1,0:T(2,128)}, u32[]{:S(2)}) copy-start(f32[2,2,768]{2,1,0:T(2,128)} %layer_scale.9) | copy-start | bytes 36868
  165.7 25.4 %copy-start = (bf16[2,256,768]{2,1,0:T(8,128)(2,1)S(1)}, bf16[2,256,768]{2,1,0:T(8,128)(2,1)}, u32[]{:S(2)}) copy-start(bf16[2,256,768]{2,1,0:T(8,128)(2,1)} %pad.30.w_out.w_out_all) | copy-start | bytes 2359300
  165.7 25.4 %copy-start.4 = (bf16[2,4,256,256]{3,2,1,0:T(8,128)(2,1)S(1)}, bf16[2,4,256,256]{3,2,1,0:T(8,128)(2,1)}, u32[]{:S(2)}) copy-start(bf16[2,4,256,256]{3,2,1,0:T(8,128)(2,1)} %get-tuple-element.58.mixture_all) | copy-start | bytes 3145732
  191.1 28.0 %copy-start.17 = (f32[8,768]{1,0:T(8,128)}, f32[8,768]{1,0:T(8,128)S(1)}, u32[]{:S(2)}) copy-start(f32[8,768]{1,0:T(8,128)S(1)} %get-tuple-element.82) | copy-start | bytes 73732
  191.1 30.4 %copy-start.3 = (f32[2,256,768]{2,1,0:T(8,128)S(1)}, f32[2,256,768]{2,1,0:T(8,128)}, u32[]{:S(2)}) copy-start(f32[2,256,768]{2,1,0:T(8,128)} %get-tuple-element.49.branch_all) | copy-start | bytes 4718596
  221.4 23.5 %copy-start.19 = (f32[8,768]{1,0:T(8,128)}, f32[8,768]{1,0:T(8,128)S(1)}, u32[]{:S(2)}) copy-start(f32[8,768]{1,0:T(8,128)S(1)} %get-tuple-element.81) | copy-start | bytes 73732
  221.4 26.8 %copy-start.16 = (f32[2,2,768]{2,1,0:T(2,128)S(1)}, f32[2,2,768]{2,1,0:T(2,128)}, u32[]{:S(2)}) copy-start(f32[2,2,768]{2,1,0:T(2,128)} %layer_scale.9) | copy-start | bytes 36868
  279.0 2.5 copy-start.6
  283.2 1.9 copy-start.28
  283.2 3.2 copy-start.24
  283.2 3.2 copy-start.22
  283.2 3.2 copy-start.18
  283.2 3.2 copy-start.20
  386.2 2.4 copy-start.26
  386.2 2.4 copy-start.43
  386.2 2.4 copy-start.44
  386.2 2.4 copy-start.45
  386.2 2.5 copy-start.42
  386.3 42.5 %copy-start.36 = (f32[256,768]{1,0:T(8,128)S(1)}, f32[256,768]{1,0:T(8,128)}, u32[]{:S(2)}) copy-start(f32[256,768]{1,0:T(8,128)} %get-tuple-element.48) | copy-start | bytes 2359300
  386.3 42.4 %copy-start.47 = (pred[256]{0:T(512)(128)(4,1)S(1)}, pred[256]{0:T(512)(128)(4,1)}, u32[]{:S(2)}) copy-start(pred[256]{0:T(512)(128)(4,1)} %copy-done.46) | copy-start | bytes 772
  546.7 3.7 copy-start.39
  546.7 3.7 copy-start.40
  546.7 4.8 copy-start.34
  546.7 4.8 copy-start.35
  551.5 2.5 copy-start.32
  551.5 2.6 copy-start.33
  (17 other events, 16.4 us)
Sparse Core Ops, SparseCore 0:
  283.3 263.3 all-reduce.9
